TPU v7x, 32 devices: a whole 2x2x4 slice. The times are simulated.
32 devices in a mesh: seq: 2 (over x), row: 16 (over z, y, core).
Axes of the slice: x: 2, y: 2, z: 4, core: 2. Of those that a mesh axis runs over, the one named last changes fastest.
Arguments:
- qm: float32 [2, 16, 7, 256, 256], P('seq', 'row'), parts along dimension 0, may hold values from 0.005 to 0.05
- qm1: float32 [2, 16, 7, 256, 256], P('seq', 'row'), parts along dimension 0, may hold values from 0.005 to 0.05
- qb: float32 [2, 16, 7, 256, 256], P('seq', 'row'), parts along dimension 0, may hold values from 0.05 to 2
- codes: int32 [2, 16, 256], P('seq', 'row'), parts along dimension 0, may hold values from 0 to 3
- energy_index: int32 [2, 16, 256, 256], P('seq', 'row'), parts along dimension 0, may hold values from 0 to 63
- turner: float32 [64], replicated, may hold values from -1 to 1.5
Outputs:
- qb_new: float32 [2, 16, 256, 256], P('seq', 'row'), parts along dimension 0
- qm1_new: float32 [2, 16, 256, 256], P('seq', 'row'), parts along dimension 0
- qm_new: float32 [2, 16, 256, 256], P('seq', 'row'), parts along dimension 0
There are 2 independent parts, one for each index of `seq`. A program takes and returns all parts, laid end to end along the dimension named above; an argument that names none is the same for every part. Nothing has to cross between parts.
All inputs are finite; a program needn't handle non-finite values.
Results may differ from a plain program's by a relative error of at most 0.0003.
Values sent between devices are 32-bit elements; how exact they have to be, the bound alone decides.
A program may use at most 64 MiB of HBM per device.

v0:
```python
import functools

import jax
import jax.numpy as jnp
from jax import lax
from jax.experimental import pallas as pl
from jax.experimental.pallas import tpu as pltpu
from jax.sharding import PartitionSpec as P

F32 = jnp.float32
BF16 = jnp.bfloat16

PLAN = {
    1: (5, (3, 4, 5, 6, 7)),
    2: (6, (2, 4, 5, 6, 7)),
    4: (8, (4, 5, 6)),
    5: (9, (3, 5, 6, 7)),
    6: (10, (2, 3, 7)),
    7: (15, (1, 2, 5, 6)),
}
CHUNKS = 2


def split(x):
    high = x.astype(BF16)
    return high, (x - high.astype(F32)).astype(BF16)


def mm(a, b):
    return jnp.dot(a, b, preferred_element_type=F32)


def dot3(a, b):
    ah, al = a
    bh, bl = b
    return mm(ah, bh) + (mm(ah, bl) + mm(al, bh))


def any_of(x, values):
    hit = x == values[0]
    for value in values[1:]:
        hit = jnp.logical_or(hit, x == value)
    return hit


def kernel(
    plan, width, qm, qm1, qb, eidx, codes, turner, acc, weight, row_sum,
    q_own, r_own, q_far, r_far, rf_h, rf_l, qb_in, e_in, code_in, acc_far, partial_in,
    own_sem, q_send, q_recv, r_send, r_recv, rf_recv, load_sem, code_sem, part_sem,
):
    dm, block = qm.shape[0], qm.shape[1]
    dist = dm + 1
    live_rows = width - dist
    beta = 1.0 / (dist * block)
    me = lax.axis_index("row")
    live = me < live_rows

    def remote(src, dst, send, recv, device):
        return pltpu.make_async_remote_copy(
            src_ref=src, dst_ref=dst, send_sem=send, recv_sem=recv,
            device_id={"row": device}, device_id_type=pl.DeviceIdType.MESH,
        )

    def moved_rows(m):
        return [row for row, (_, shifts) in plan.items() if m in shifts]

    def own(m):
        rows = moved_rows(m)
        return jnp.logical_and(live, jnp.logical_not(any_of(me, rows))) if rows else live

    def direct(m):
        row = me - m
        ok = jnp.logical_and(row >= 0, row < live_rows)
        rows = moved_rows(m)
        return jnp.logical_and(ok, jnp.logical_not(any_of(row, rows))) if rows else ok

    def code_send():
        return remote(codes, code_in, code_sem.at[0], code_sem.at[1], me - dist)

    height = block // CHUNKS

    def rows_of(c):
        return pl.ds(c * height, height)

    def q_copy(m, c, device):
        at = (m - 1, rows_of(c))
        return remote(qm.at[at], q_far.at[at], q_send.at[m - 1, c], q_recv.at[m - 1, c], device)

    def r_copy(m, device):
        return remote(qm1.at[dm - m], r_own.at[m - 1], r_send.at[m - 1], r_recv.at[m - 1], device)

    def rf_copy(m, device):
        return remote(qm1.at[dm - m], r_far.at[m - 1], r_send.at[m - 1], rf_recv.at[m - 1], device)

    def part_copy(c, device):
        at = pl.ds(c * height, height + (8 if c == CHUNKS - 1 else 0))
        return remote(acc_far.at[at], partial_in.at[at], part_sem.at[0, c], part_sem.at[1, c], device)

    barrier = pltpu.get_barrier_semaphore()

    def greet(device):
        pl.semaphore_signal(
            barrier, inc=1, device_id={"row": device}, device_id_type=pl.DeviceIdType.MESH
        )

    extra = set()
    for row, (device, shifts) in plan.items():
        extra |= {(row, device), (device, row)} | {(row + m, device) for m in shifts}
    extra = sorted((s, d) for s, d in extra if s != d and not (d < live_rows and 1 <= s - d <= dist))

    @pl.when(live)
    def _():
        for m in range(1, dist + 1):
            greet(me + m)

    for source, device in extra:

        @pl.when(me == device)
        def _():
            greet(source)

    awaited = jnp.int32(0)
    for m in range(1, dist + 1):
        row = me - m
        awaited = awaited + jnp.where(jnp.logical_and(row >= 0, row < live_rows), 1, 0)
    for source, _ in extra:
        awaited = awaited + jnp.where(me == source, 1, 0)

    @pl.when(awaited > 0)
    def _():
        pl.semaphore_wait(barrier, awaited)

    @pl.when(me >= dist)
    def _():
        code_send().start()

    for m in range(dm, 0, -1):
        for row in moved_rows(m):
            device = plan[row][0]

            if row + m == device:

                @pl.when(me == device)
                def _():
                    pltpu.make_async_copy(qm1.at[dm - m], r_far.at[m - 1], rf_recv.at[m - 1]).start()

            else:

                @pl.when(me == row + m)
                def _():
                    rf_copy(m, device).start()

    for row, (device, shifts) in plan.items():

        @pl.when(me == row)
        def _():
            for c in range(CHUNKS):
                for m in reversed(shifts):
                    q_copy(m, c, device).start()

    for m in range(dm, 0, -1):

        @pl.when(direct(m))
        def _():
            r_copy(m, me - m).start()

    loads = (
        pltpu.make_async_copy(qb, qb_in, load_sem.at[0]),
        pltpu.make_async_copy(eidx, e_in, load_sem.at[1]),
    )

    @pl.when(live)
    def _():
        for load in loads:
            load.start()

    for m in range(1, dist):

        @pl.when(own(m))
        def _():
            pltpu.make_async_copy(qm.at[m - 1], q_own.at[m - 1], own_sem.at[m - 1]).start()

    acc[...] = jnp.zeros_like(acc)
    acc_far[...] = jnp.zeros_like(acc_far)
    rows_i = lax.broadcasted_iota(jnp.int32, (block, block), 0)
    cols_i = lax.broadcasted_iota(jnp.int32, (block, block), 1)
    column = lax.broadcasted_iota(jnp.int32, (block, 1), 0)
    line = lax.broadcasted_iota(jnp.int32, (1, block), 1)

    @pl.when(live)
    def _():
        code_send().wait_recv()
        first = jnp.sum(jnp.where(rows_i == cols_i, codes[...].astype(F32), 0.0), axis=1, keepdims=True)
        both = first + code_in[...].astype(F32)
        allowed = jnp.where(jnp.logical_or(both == 3.0, both == 5.0), 1.0, 0.0)
        table = jnp.exp(-turner[...])
        entries = table.shape[1]
        table = jnp.concatenate([table, jnp.zeros((1, 128 - entries), F32)], axis=1)
        table = jnp.broadcast_to(table, (block, 128))
        loads[1].wait()
        for start in range(0, block, 128):
            part = pl.ds(start, 128)
            found = jnp.take_along_axis(table, e_in[:, part], axis=1, mode="promise_in_bounds")
            weight[:, part] = found * allowed[:, start : start + 128]
        loads[0].wait()
        total = jnp.zeros((block, block), F32)
        for e in range(1, dist):
            factor = jnp.exp((line - (dist - e) * block).astype(F32) * beta)
            total = total + qb_in[e - 1] * factor
        row_sum[...] = jnp.broadcast_to(jnp.sum(total, axis=1, keepdims=True), row_sum.shape)

    def column_sum(m, right, total):
        fade = jnp.exp((-(m + 1) * block - column).astype(F32) * beta)
        total[block : block + 1, :] += jnp.sum(right * fade, axis=0, keepdims=True)

    def mask_of(cases):
        total = jnp.int32(0)
        for device, shifts in cases:
            total = total + jnp.where(me == device, sum(2 ** (dm - m) for m in shifts), 0)
        return total

    if plan:
        far_mask = mask_of(list(plan.values()))
        for c in range(CHUNKS):
            at = rows_of(c)

            def far_step(step, rest):
                m = dm - 1 - step

                @pl.when(rest % 2 == 1)
                def _():
                    if c == 0:
                        rf_copy(m + 1, 0).wait_recv()
                        right = r_far[m]
                        rf_h[m], rf_l[m] = split(right)
                        column_sum(m, right, acc_far)
                    q_copy(m + 1, c, 0).wait_recv()
                    acc_far[at, :] += dot3(split(q_far[m, at, :]), (rf_h[m], rf_l[m]))

                return rest // 2

            lax.fori_loop(0, dm, far_step, far_mask)
            for row, (device, _) in plan.items():

                @pl.when(me == device)
                def _():
                    part_copy(c, row).start()

    moved = mask_of([(row, shifts) for row, (_, shifts) in plan.items()])
    own_mask = jnp.where(live, 2**dm - 1 - moved, 0)

    def own_step(step, rest):
        m = dm - 1 - step

        @pl.when(rest % 2 == 1)
        def _():
            pltpu.make_async_copy(qm.at[m], q_own.at[m], own_sem.at[m]).wait()
            r_copy(m + 1, 0).wait_recv()
            right = r_own[m]
            column_sum(m, right, acc)
            acc[0:block, :] += dot3(split(q_own[m]), split(right))

        return rest // 2

    lax.fori_loop(0, dm, own_step, own_mask)

    if plan:

        @pl.when(any_of(me, list(plan)))
        def _():
            for c in range(CHUNKS):
                part_copy(c, 0).wait_recv()
            acc[...] += partial_in[...]

    for m in range(1, dist):
        rows = moved_rows(m)
        row = me - m

        @pl.when(jnp.logical_and(row >= 0, row < live_rows))
        def _():
            if rows and any(plan[r][0] == r + m for r in rows):
                stays = any_of(me, [r + m for r in rows if plan[r][0] == r + m])

                @pl.when(jnp.logical_not(stays))
                def _():
                    r_copy(m, 0).wait_send()

            else:
                r_copy(m, 0).wait_send()

        if rows:

            @pl.when(any_of(me, rows))
            def _():
                for c in range(CHUNKS):
                    q_copy(m, c, 0).wait_send()

    @pl.when(me >= dist)
    def _():
        code_send().wait_send()

    if plan:

        @pl.when(any_of(me, [device for device, _ in plan.values()]))
        def _():
            for c in range(CHUNKS):
                part_copy(c, 0).wait_send()


def finish(live_rows, dist, acc, weight, row_sum, pair_out, branch_out, multi_out):
    block = weight.shape[0]
    beta = 1.0 / (dist * block)
    live = lax.axis_index("row") < live_rows

    @pl.when(live)
    def _():
        column = lax.broadcasted_iota(jnp.int32, (block, 1), 0).astype(F32)
        line = lax.broadcasted_iota(jnp.int32, (1, block), 1).astype(F32)
        rows_i = lax.broadcasted_iota(jnp.int32, (block, block), 0)
        cols_i = lax.broadcasted_iota(jnp.int32, (block, block), 1)
        upper = jnp.where(cols_i >= rows_i, 1.0, 0.0).astype(BF16)
        summed = acc[0:block, :]
        pair = weight[...] * (1.0 + 0.8 * summed)
        pair_out[...] = pair
        high, low = split(pair * jnp.exp(line * beta))
        inner = mm(high, upper) + mm(low, upper)
        branch = (row_sum[:, 0:1] + inner) * (beta * jnp.exp(line * (-beta)))
        branch_out[...] = branch
        high, low = split(branch * jnp.exp(column * (-beta)))
        tails = acc[block : block + 1, :] + mm(upper, high) + mm(upper, low)
        multi_out[...] = summed + 0.01 * jnp.exp(column * beta) * tails

    @pl.when(jnp.logical_not(live))
    def _():
        for out in (pair_out, branch_out, multi_out):
            out[...] = jnp.zeros_like(out)


def solution(mesh):
    width = mesh.shape["row"]

    def per_device(qm, qm1, qb, codes, energy_index, turner):
        dm, block = qm.shape[2], qm.shape[3]
        dist = dm + 1
        plan = PLAN if width == 16 and dist == 8 else {}
        blocks = pltpu.VMEM((dm, block, block), F32)
        halves = pltpu.VMEM((dm, block, block), BF16)
        square = jax.ShapeDtypeStruct((block, block), F32)
        tall = pltpu.VMEM((block + 8, block), F32)
        dma = pltpu.SemaphoreType.DMA
        anywhere = pl.BlockSpec(memory_space=pltpu.HBM)
        local = pl.BlockSpec(memory_space=pltpu.VMEM)
        middle = pl.pallas_call(
            functools.partial(kernel, plan, width),
            out_shape=[
                pltpu.VMEM((block + 8, block), F32),
                pltpu.VMEM((block, block), F32),
                pltpu.VMEM((block, 128), F32),
            ],
            in_specs=[anywhere] * 4 + [local] * 2,
            out_specs=[local] * 3,
            scratch_shapes=[
                blocks, blocks, blocks, blocks, halves, halves, blocks,
                pltpu.VMEM((block, block), jnp.int32),
                pltpu.VMEM((1, block), jnp.int32),
                tall, tall,
                dma((dm,)), dma((dm, CHUNKS)), dma((dm, CHUNKS)), dma((dm,)), dma((dm,)), dma((dm,)),
                dma((2,)), dma((2,)), dma((2, CHUNKS)),
            ],
            compiler_params=pltpu.CompilerParams(has_side_effects=True, collective_id=0),
        )(
            qm[0, 0], qm1[0, 0], qb[0, 0], energy_index[0, 0],
            codes[0], turner[None, :],
        )
        outs = pl.pallas_call(
            functools.partial(finish, width - dist, dist),
            out_shape=[square] * 3,
            in_specs=[local] * 3,
            out_specs=[local] * 3,
            compiler_params=pltpu.CompilerParams(vmem_limit_bytes=16 * 2**20),
        )(*middle)
        return tuple(out[None, None] for out in outs)

    return jax.shard_map(
        per_device,
        mesh=mesh,
        in_specs=(
            P("seq", "row", None, None, None),
            P("seq", "row", None, None, None),
            P("seq", "row", None, None, None),
            P("seq", "row", None),
            P("seq", "row", None, None),
            P(),
        ),
        out_specs=(
            P("seq", "row", None, None),
            P("seq", "row", None, None),
            P("seq", "row", None, None),
        ),
        check_vma=False,
    )
```

profile of v0, /device:TPU:8, one launch (start us, length us, event | category | flops | bytes accessed | tf_op | source)
XLA Modules:
  0.0 33.6 jit_solution(10473073273546287861)
XLA Ops:
  0.6 31.6 %shard_map.85 = (f32[264,256]{1,0:T(8,128)S(1)}, f32[256,256]{1,0:T(8,128)S(1)}, f32[256,128]{1,0:T(8,128)S(1)}) custom-call(f32[7,256,256]{2,1,0:T(8,128)} %bitcast.9, f32[7,256,256]{2,1,0:T(8,128)} %bitcast.10, f32[7,256,256]{2,1,0:T(8,128)} %bitcast.11, s32[256,256]{1,0:T(8,128)} %bitcast.12, s32[1,256]{1,0:T(1,128)} %bitcast.13, f32[1,64]{1,0:T(1,128)} %bitcast.14), custom_call_target="tpu_custom_call" | custom-call | tf_op jit(solution)/shard_map/pallas_call | solution.py:353
  32.2 1.4 %shard_map.86 = (f32[256,256]{1,0:T(8,128)}, f32[256,256]{1,0:T(8,128)}, f32[256,256]{1,0:T(8,128)}) custom-call(f32[264,256]{1,0:T(8,128)S(1)} %get-tuple-element.9.acc, f32[256,256]{1,0:T(8,128)S(1)} %get-tuple-element.10.weight, f32[256,128]{1,0:T(8,128)S(1)} %get-tuple-element.11.row_sum), custom_call_target="tpu_custom_call" | custom-call | tf_op jit(solution)/shard_map/pallas_call | solution.py:375
where the time goes:
time: 33.8 us; the launch traced here: 33.6 us
  Pallas kernels  33 us (98%)
  between operations  0.64 us (2%)
    pallas_call x1, Pallas kernels, per_device(): pl.pallas_call(functools.partial(kernel, plan, width), out_shape=[pltpu.V...  31.6 us
    pallas_call x1, Pallas kernels, per_device(): pl.pallas_call(functools.partial(finish, width - dist, dist), out_shape=[...  1.44 us

commit v1 on v0

--- a/solution.py
+++ b/solution.py
@@ -11,14 +11,19 @@
 BF16 = jnp.bfloat16
 
 PLAN = {
-    1: (5, (3, 4, 5, 6, 7)),
-    2: (6, (2, 4, 5, 6, 7)),
-    4: (8, (4, 5, 6)),
-    5: (9, (3, 5, 6, 7)),
-    6: (10, (2, 3, 7)),
-    7: (15, (1, 2, 5, 6)),
+    1: (5, (3, 4, 6, 7)),
+    3: (7, (1, 2, 3, 4, 5, 6, 7)),
+    4: (8, (4, 5)),
+    5: (9, (3, 4, 5, 6, 7)),
+    7: (11, (1, 2, 3, 4, 5, 6, 7)),
 }
-CHUNKS = 2
+RELAY = {
+    (6, 7): (15, 4),
+    (6, 6): (14, 4),
+    (3, 6): (11, 2),
+}
+CHUNKS = 4
+PIECES = 4
 
 
 def split(x):
@@ -44,9 +49,9 @@
 
 
 def kernel(
-    plan, width, qm, qm1, qb, eidx, codes, turner, acc, weight, row_sum,
-    q_own, r_own, q_far, r_far, rf_h, rf_l, qb_in, e_in, code_in, acc_far, partial_in,
-    own_sem, q_send, q_recv, r_send, r_recv, rf_recv, load_sem, code_sem, part_sem,
+    plan, relay, width, qm, qm1, qb, eidx, codes, turner, acc, weight, row_sum,
+    q_own, r_own, q_far, r_far, rf_h, rf_l, qb_in, e_in, code_in, acc_far, partial_in, relay_in,
+    own_sem, q_send, q_recv, r_send, r_recv, rf_recv, load_sem, code_sem, part_sem, relay_sem,
 ):
     dm, block = qm.shape[0], qm.shape[1]
     dist = dm + 1
@@ -64,6 +69,13 @@
     def moved_rows(m):
         return [row for row, (_, shifts) in plan.items() if m in shifts]
 
+    def home(row, m):
+        device, shifts = plan.get(row, (None, ()))
+        return (device, r_far, rf_recv) if m in shifts else (row, r_own, r_recv)
+
+    def relayed(m):
+        return sorted(row for row, shift in relay if shift == m)
+
     def own(m):
         rows = moved_rows(m)
         return jnp.logical_and(live, jnp.logical_not(any_of(me, rows))) if rows else live
@@ -71,7 +83,7 @@
     def direct(m):
         row = me - m
         ok = jnp.logical_and(row >= 0, row < live_rows)
-        rows = moved_rows(m)
+        rows = moved_rows(m) + relayed(m)
         return jnp.logical_and(ok, jnp.logical_not(any_of(row, rows))) if rows else ok
 
     def code_send():
@@ -91,6 +103,22 @@
 
     def rf_copy(m, device):
         return remote(qm1.at[dm - m], r_far.at[m - 1], r_send.at[m - 1], rf_recv.at[m - 1], device)
+
+    piece = block // PIECES
+
+    def relay_copy(m, p, device):
+        at = pl.ds(p * piece, piece)
+        return remote(qm1.at[dm - m, at], relay_in.at[at], r_send.at[m - 1], relay_sem.at[0, p], device)
+
+    def relay_on(row, m, p):
+        device, target, sem = home(row, m)
+        at = pl.ds(p * piece, piece)
+        return remote(relay_in.at[at], target.at[m - 1, at], relay_sem.at[1, p], sem.at[m - 1], device)
+
+    def relay_rest(row, m, count):
+        device, target, sem = home(row, m)
+        at = pl.ds(count * piece, block - count * piece)
+        return remote(qm1.at[dm - m, at], target.at[m - 1, at], r_send.at[m - 1], sem.at[m - 1], device)
 
     def part_copy(c, device):
         at = pl.ds(c * height, height + (8 if c == CHUNKS - 1 else 0))
@@ -106,6 +134,8 @@
     extra = set()
     for row, (device, shifts) in plan.items():
         extra |= {(row, device), (device, row)} | {(row + m, device) for m in shifts}
+    for (row, m), (via, _) in relay.items():
+        extra |= {(row + m, via), (via, home(row, m)[0])}
     extra = sorted((s, d) for s, d in extra if s != d and not (d < live_rows and 1 <= s - d <= dist))
 
     @pl.when(live)
@@ -134,9 +164,20 @@
     def _():
         code_send().start()
 
+    for (row, m), (via, count) in relay.items():
+
+        @pl.when(me == row + m)
+        def _():
+            for p in range(count):
+                relay_copy(m, p, via).start()
+            if count < PIECES:
+                relay_rest(row, m, count).start()
+
     for m in range(dm, 0, -1):
         for row in moved_rows(m):
             device = plan[row][0]
+            if (row, m) in relay:
+                continue
 
             if row + m == device:
 
@@ -179,6 +220,14 @@
         @pl.when(own(m))
         def _():
             pltpu.make_async_copy(qm.at[m - 1], q_own.at[m - 1], own_sem.at[m - 1]).start()
+
+    for (row, m), (via, count) in relay.items():
+
+        @pl.when(me == via)
+        def _():
+            for p in range(count):
+                relay_copy(m, p, 0).wait_recv()
+                relay_on(row, m, p).start()
 
     acc[...] = jnp.zeros_like(acc)
     acc_far[...] = jnp.zeros_like(acc_far)
@@ -306,6 +355,13 @@
             for c in range(CHUNKS):
                 part_copy(c, 0).wait_send()
 
+    for (row, m), (via, count) in relay.items():
+
+        @pl.when(me == via)
+        def _():
+            for p in range(count):
+                relay_on(row, m, p).wait_send()
+
 
 def finish(live_rows, dist, acc, weight, row_sum, pair_out, branch_out, multi_out):
     block = weight.shape[0]
@@ -342,7 +398,9 @@
     def per_device(qm, qm1, qb, codes, energy_index, turner):
         dm, block = qm.shape[2], qm.shape[3]
         dist = dm + 1
-        plan = PLAN if width == 16 and dist == 8 else {}
+        known = width == 16 and dist == 8
+        plan = PLAN if known else {}
+        relay = RELAY if known else {}
         blocks = pltpu.VMEM((dm, block, block), F32)
         halves = pltpu.VMEM((dm, block, block), BF16)
         square = jax.ShapeDtypeStruct((block, block), F32)
@@ -351,7 +409,7 @@
         anywhere = pl.BlockSpec(memory_space=pltpu.HBM)
         local = pl.BlockSpec(memory_space=pltpu.VMEM)
         middle = pl.pallas_call(
-            functools.partial(kernel, plan, width),
+            functools.partial(kernel, plan, relay, width),
             out_shape=[
                 pltpu.VMEM((block + 8, block), F32),
                 pltpu.VMEM((block, block), F32),
@@ -363,9 +421,9 @@
                 blocks, blocks, blocks, blocks, halves, halves, blocks,
                 pltpu.VMEM((block, block), jnp.int32),
                 pltpu.VMEM((1, block), jnp.int32),
-                tall, tall,
+                tall, tall, pltpu.VMEM((block, block), F32),
                 dma((dm,)), dma((dm, CHUNKS)), dma((dm, CHUNKS)), dma((dm,)), dma((dm,)), dma((dm,)),
-                dma((2,)), dma((2,)), dma((2, CHUNKS)),
+                dma((2,)), dma((2,)), dma((2, CHUNKS)), dma((2, PIECES)),
             ],
             compiler_params=pltpu.CompilerParams(has_side_effects=True, collective_id=0),
         )(

time: 33.8 us -> 35.8 us (1.059)
  the two profiles are of different devices: /device:TPU:8 before, /device:TPU:5 now
where the time goes in v1:
time: 35.8 us; the launch traced here: 35.6 us
  Pallas kernels  34.9 us (97%)
  between operations  0.64 us (2%)
    pallas_call x1, Pallas kernels, per_device(): pl.pallas_call(functools.partial(kernel, plan, relay, width), out_shape=[...  33.5 us
    pallas_call x1, Pallas kernels, per_device(): pl.pallas_call(functools.partial(finish, width - dist, dist), out_shape=[...  1.44 us

profile of v1, /device:TPU:5, one launch (start us, length us, event | category | flops | bytes accessed | tf_op | source)
XLA Modules:
  0.0 35.6 jit_solution(4281682456289846943)
XLA Ops:
  0.6 33.5 %shard_map.85 = (f32[264,256]{1,0:T(8,128)S(1)}, f32[256,256]{1,0:T(8,128)S(1)}, f32[256,128]{1,0:T(8,128)S(1)}) custom-call(f32[7,256,256]{2,1,0:T(8,128)} %bitcast.9, f32[7,256,256]{2,1,0:T(8,128)} %bitcast.10, f32[7,256,256]{2,1,0:T(8,128)} %bitcast.11, s32[256,256]{1,0:T(8,128)} %bitcast.12, s32[1,256]{1,0:T(1,128)} %bitcast.13, f32[1,64]{1,0:T(1,128)} %bitcast.14), custom_call_target="tpu_custom_call" | custom-call | tf_op jit(solution)/shard_map/pallas_call | solution.py:411
  34.1 1.4 %shard_map.86 = (f32[256,256]{1,0:T(8,128)}, f32[256,256]{1,0:T(8,128)}, f32[256,256]{1,0:T(8,128)}) custom-call(f32[264,256]{1,0:T(8,128)S(1)} %get-tuple-element.9.acc, f32[256,256]{1,0:T(8,128)S(1)} %get-tuple-element.10.weight, f32[256,128]{1,0:T(8,128)S(1)} %get-tuple-element.11.row_sum), custom_call_target="tpu_custom_call" | custom-call | tf_op jit(solution)/shard_map/pallas_call | solution.py:433

commit v2 on v1

--- a/solution.py
+++ b/solution.py
@@ -13,16 +13,17 @@
 PLAN = {
     1: (5, (3, 4, 6, 7)),
     3: (7, (1, 2, 3, 4, 5, 6, 7)),
-    4: (8, (4, 5)),
+    4: (8, (4, 5, 6)),
     5: (9, (3, 4, 5, 6, 7)),
     7: (11, (1, 2, 3, 4, 5, 6, 7)),
 }
 RELAY = {
     (6, 7): (15, 4),
     (6, 6): (14, 4),
-    (3, 6): (11, 2),
+    (6, 2): (10, 4),
 }
-CHUNKS = 4
+SHARES = (4, 2, 1, 1)
+CHUNKS = len(SHARES)
 PIECES = 4
 
 
@@ -50,7 +51,7 @@
 
 def kernel(
     plan, relay, width, qm, qm1, qb, eidx, codes, turner, acc, weight, row_sum,
-    q_own, r_own, q_far, r_far, rf_h, rf_l, qb_in, e_in, code_in, acc_far, partial_in, relay_in,
+    q_own, r_own, q_far, r_far, rf_h, rf_l, qb_in, e_in, code_in, acc_far, partial_in, relay_in, code_own, table_in,
     own_sem, q_send, q_recv, r_send, r_recv, rf_recv, load_sem, code_sem, part_sem, relay_sem,
 ):
     dm, block = qm.shape[0], qm.shape[1]
@@ -89,10 +90,10 @@
     def code_send():
         return remote(codes, code_in, code_sem.at[0], code_sem.at[1], me - dist)
 
-    height = block // CHUNKS
-
-    def rows_of(c):
-        return pl.ds(c * height, height)
+    unit = block // sum(SHARES)
+
+    def rows_of(c, more=0):
+        return pl.ds(sum(SHARES[:c]) * unit, SHARES[c] * unit + more)
 
     def q_copy(m, c, device):
         at = (m - 1, rows_of(c))
@@ -121,7 +122,7 @@
         return remote(qm1.at[dm - m, at], target.at[m - 1, at], r_send.at[m - 1], sem.at[m - 1], device)
 
     def part_copy(c, device):
-        at = pl.ds(c * height, height + (8 if c == CHUNKS - 1 else 0))
+        at = rows_of(c, 8 if c == CHUNKS - 1 else 0)
         return remote(acc_far.at[at], partial_in.at[at], part_sem.at[0, c], part_sem.at[1, c], device)
 
     barrier = pltpu.get_barrier_semaphore()
@@ -164,15 +165,6 @@
     def _():
         code_send().start()
 
-    for (row, m), (via, count) in relay.items():
-
-        @pl.when(me == row + m)
-        def _():
-            for p in range(count):
-                relay_copy(m, p, via).start()
-            if count < PIECES:
-                relay_rest(row, m, count).start()
-
     for m in range(dm, 0, -1):
         for row in moved_rows(m):
             device = plan[row][0]
@@ -191,6 +183,15 @@
                 def _():
                     rf_copy(m, device).start()
 
+    for (row, m), (via, count) in relay.items():
+
+        @pl.when(me == row + m)
+        def _():
+            for p in range(count):
+                relay_copy(m, p, via).start()
+            if count < PIECES:
+                relay_rest(row, m, count).start()
+
     for row, (device, shifts) in plan.items():
 
         @pl.when(me == row)
@@ -208,6 +209,8 @@
     loads = (
         pltpu.make_async_copy(qb, qb_in, load_sem.at[0]),
         pltpu.make_async_copy(eidx, e_in, load_sem.at[1]),
+        pltpu.make_async_copy(codes, code_own, load_sem.at[2]),
+        pltpu.make_async_copy(turner, table_in, load_sem.at[3]),
     )
 
     @pl.when(live)
@@ -239,10 +242,12 @@
     @pl.when(live)
     def _():
         code_send().wait_recv()
-        first = jnp.sum(jnp.where(rows_i == cols_i, codes[...].astype(F32), 0.0), axis=1, keepdims=True)
+        loads[2].wait()
+        loads[3].wait()
+        first = jnp.sum(jnp.where(rows_i == cols_i, code_own[...].astype(F32), 0.0), axis=1, keepdims=True)
         both = first + code_in[...].astype(F32)
         allowed = jnp.where(jnp.logical_or(both == 3.0, both == 5.0), 1.0, 0.0)
-        table = jnp.exp(-turner[...])
+        table = jnp.exp(-table_in[...])
         entries = table.shape[1]
         table = jnp.concatenate([table, jnp.zeros((1, 128 - entries), F32)], axis=1)
         table = jnp.broadcast_to(table, (block, 128))
@@ -415,15 +420,17 @@
                 pltpu.VMEM((block, block), F32),
                 pltpu.VMEM((block, 128), F32),
             ],
-            in_specs=[anywhere] * 4 + [local] * 2,
+            in_specs=[anywhere] * 6,
             out_specs=[local] * 3,
             scratch_shapes=[
                 blocks, blocks, blocks, blocks, halves, halves, blocks,
                 pltpu.VMEM((block, block), jnp.int32),
                 pltpu.VMEM((1, block), jnp.int32),
                 tall, tall, pltpu.VMEM((block, block), F32),
+                pltpu.VMEM((1, block), jnp.int32),
+                pltpu.VMEM((1, turner.shape[0]), F32),
                 dma((dm,)), dma((dm, CHUNKS)), dma((dm, CHUNKS)), dma((dm,)), dma((dm,)), dma((dm,)),
-                dma((2,)), dma((2,)), dma((2, CHUNKS)), dma((2, PIECES)),
+                dma((4,)), dma((2,)), dma((2, CHUNKS)), dma((2, PIECES)),
             ],
             compiler_params=pltpu.CompilerParams(has_side_effects=True, collective_id=0),
         )(

time: 35.8 us -> 31.7 us (0.89)
  the two profiles are of different devices: /device:TPU:5 before, /device:TPU:9 now
where the time goes in v2:
time: 31.7 us; the launch traced here: 31.6 us
  Pallas kernels  30.9 us (97%)
  between operations  0.64 us (2%)
    pallas_call x1, Pallas kernels, per_device(): pl.pallas_call(functools.partial(kernel, plan, relay, width), out_shape=[...  29.5 us
    pallas_call x1, Pallas kernels, per_device(): pl.pallas_call(functools.partial(finish, width - dist, dist), out_shape=[...  1.44 us

profile of v2, /device:TPU:9, one launch (start us, length us, event | category | flops | bytes accessed | tf_op | source)
XLA Modules:
  0.0 31.6 jit_solution(9674569479642514573)
XLA Ops:
  0.6 29.5 %shard_map.85 = (f32[264,256]{1,0:T(8,128)S(1)}, f32[256,256]{1,0:T(8,128)S(1)}, f32[256,128]{1,0:T(8,128)S(1)}) custom-call(f32[7,256,256]{2,1,0:T(8,128)} %bitcast.9, f32[7,256,256]{2,1,0:T(8,128)} %bitcast.10, f32[7,256,256]{2,1,0:T(8,128)} %bitcast.11, s32[256,256]{1,0:T(8,128)} %bitcast.12, s32[1,256]{1,0:T(1,128)} %bitcast.13, f32[1,64]{1,0:T(1,128)} %bitcast.14), custom_call_target="tpu_custom_call" | custom-call | tf_op jit(solution)/shard_map/pallas_call | solution.py:416
  30.1 1.4 %shard_map.86 = (f32[256,256]{1,0:T(8,128)}, f32[256,256]{1,0:T(8,128)}, f32[256,256]{1,0:T(8,128)}) custom-call(f32[264,256]{1,0:T(8,128)S(1)} %get-tuple-element.9.acc, f32[256,256]{1,0:T(8,128)S(1)} %get-tuple-element.10.weight, f32[256,128]{1,0:T(8,128)S(1)} %get-tuple-element.11.row_sum), custom_call_target="tpu_custom_call" | custom-call | tf_op jit(solution)/shard_map/pallas_call | solution.py:440

commit v3 on v0

v3 whole, which is shorter than its diff:
```python
import functools

import jax
import jax.numpy as jnp
from jax import lax
from jax.experimental import pallas as pl
from jax.experimental.pallas import tpu as pltpu
from jax.sharding import PartitionSpec as P

F32 = jnp.float32
BF16 = jnp.bfloat16

PLAN = {
    1: (5, (4, 3, 6, 5, 7)),
    3: (7, (4, 3, 1, 2, 6, 5, 7)),
    4: (8, (7, 6)),
    5: (9, (4, 3, 6, 5, 7)),
    7: (11, (4, 3, 7, 5, 6, 2, 1)),
}
RELAY = {
    (6, 7): (15, 2),
    (6, 6): (14, 2),
    (2, 7): (10, 2),
    (6, 3): (10, 2),
    (6, 2): (10, 1),
}
LATE = ((6, 2),)
ORDER = {6: (1, 5, 4, 7, 6, 3, 2)}
SHARES = (4, 2, 1, 1)
CHUNKS = len(SHARES)
PIECES = 2


def split(x):
    high = x.astype(BF16)
    return high, (x - high.astype(F32)).astype(BF16)


def mm(a, b):
    return jnp.dot(a, b, preferred_element_type=F32)


def dot3(a, b):
    ah, al = a
    bh, bl = b
    return mm(ah, bh) + (mm(ah, bl) + mm(al, bh))


def any_of(x, values):
    hit = x == values[0]
    for value in values[1:]:
        hit = jnp.logical_or(hit, x == value)
    return hit


def kernel(
    plan, relay, order, width, qm, qm1, qb, eidx, codes, turner, acc, weight, row_sum,
    q_own, r_in, q_far, rf_h, rf_l, qb_in, e_in, code_in, acc_far, partial_in, relay_in, code_own, table_in,
    own_sem, q_send, q_recv, r_send, r_recv, load_sem, code_sem, part_sem, relay_send, relay_recv,
):
    dm, block = qm.shape[0], qm.shape[1]
    dist = dm + 1
    live_rows = width - dist
    beta = 1.0 / (dist * block)
    base = dm + 1
    me = lax.axis_index("row")
    live = me < live_rows
    unit = block // sum(SHARES)
    piece = block // PIECES

    def remote(src, dst, send, recv, device):
        return pltpu.make_async_remote_copy(
            src_ref=src, dst_ref=dst, send_sem=send, recv_sem=recv,
            device_id={"row": device}, device_id_type=pl.DeviceIdType.MESH,
        )

    def home(row, m):
        device, shifts = plan.get(row, (None, ()))
        return device if m in shifts else row

    def apart(m):
        return [row for row in range(live_rows) if (row, m) in relay or home(row, m) != row] if plan else []

    def direct(m):
        row = me - m
        ok = jnp.logical_and(row >= 0, row < live_rows)
        rows = apart(m)
        return jnp.logical_and(ok, jnp.logical_not(any_of(row, rows))) if rows else ok

    def code_send():
        return remote(codes, code_in, code_sem.at[0], code_sem.at[1], me - dist)

    def rows_of(c, more=0):
        return pl.ds(sum(SHARES[:c]) * unit, SHARES[c] * unit + more)

    def q_copy(m, c, device):
        at = (m - 1, rows_of(c))
        slot = c if c < CHUNKS - 1 else CHUNKS - 2 + m
        return remote(qm.at[at], q_far.at[at], q_send.at[0], q_recv.at[slot], device)

    def r_copy(m, device):
        return remote(qm1.at[dm - m], r_in.at[m - 1], r_send.at[0], r_recv.at[m - 1], device)

    slots = {}
    for (row, m), (via, count) in relay.items():
        for p in range(count):
            slots[row, m, p] = sum(1 for key in slots if relay[key[:2]][0] == via)

    def relay_copy(row, m, p):
        slot = slots[row, m, p]
        return remote(
            qm1.at[dm - m, pl.ds(p * piece, piece)], relay_in.at[slot],
            r_send.at[0], relay_recv.at[slot], relay[row, m][0],
        )

    def relay_on(row, m, p):
        at = pl.ds(p * piece, piece)
        return remote(
            relay_in.at[slots[row, m, p]], r_in.at[m - 1, at],
            relay_send.at[0], r_recv.at[m - 1], home(row, m),
        )

    def relay_rest(row, m):
        start = relay[row, m][1] * piece
        at = pl.ds(start, block - start)
        return remote(
            qm1.at[dm - m, at], r_in.at[m - 1, at], r_send.at[0], r_recv.at[m - 1], home(row, m)
        )

    def part_copy(c, device):
        at = rows_of(c, 8 if c == CHUNKS - 1 else 0)
        return remote(acc_far.at[at], partial_in.at[at], part_sem.at[0], part_sem.at[1], device)

    barrier = pltpu.get_barrier_semaphore()

    def greet(device):
        pl.semaphore_signal(
            barrier, inc=1, device_id={"row": device}, device_id_type=pl.DeviceIdType.MESH
        )

    extra = set()
    for row, (device, shifts) in plan.items():
        extra |= {(row, device), (device, row)} | {(row + m, device) for m in shifts}
    for (row, m), (via, _) in relay.items():
        extra |= {(row + m, via), (via, home(row, m))}
    extra = sorted((s, d) for s, d in extra if s != d and not (d < live_rows and 1 <= s - d <= dist))

    @pl.when(live)
    def _():
        for m in range(1, dist + 1):
            greet(me + m)

    for device in sorted({d for _, d in extra}):

        @pl.when(me == device)
        def _():
            for source in [s for s, d in extra if d == device]:
                greet(source)

    awaited = jnp.int32(0)
    for m in range(1, dist + 1):
        row = me - m
        awaited = awaited + jnp.where(jnp.logical_and(row >= 0, row < live_rows), 1, 0)
    for source in sorted({s for s, _ in extra}):
        awaited = awaited + jnp.where(me == source, sum(1 for s, _ in extra if s == source), 0)

    @pl.when(awaited > 0)
    def _():
        pl.semaphore_wait(barrier, awaited)

    @pl.when(me >= dist)
    def _():
        code_send().start()

    for m in range(dm, 0, -1):
        for row, (device, shifts) in plan.items():
            if m not in shifts or (row, m) in relay:
                continue

            @pl.when(me == row + m)
            def _():
                if row + m == device:
                    pltpu.make_async_copy(qm1.at[dm - m], r_in.at[m - 1], r_recv.at[m - 1]).start()
                else:
                    r_copy(m, device).start()

    for row, (device, shifts) in plan.items():

        @pl.when(me == row)
        def _():
            for c in range(CHUNKS):
                for m in shifts:
                    q_copy(m, c, device).start()

    for (row, m), (via, count) in relay.items():

        @pl.when(me == row + m)
        def _():
            for p in range(count):
                relay_copy(row, m, p).start()
            if count < PIECES and (row, m) not in LATE:
                relay_rest(row, m).start()

    for m in range(dm, 0, -1):

        @pl.when(direct(m))
        def _():
            r_copy(m, me - m).start()

    loads = (
        pltpu.make_async_copy(qb, qb_in, load_sem.at[0]),
        pltpu.make_async_copy(eidx, e_in, load_sem.at[1]),
        pltpu.make_async_copy(codes, code_own, load_sem.at[2]),
        pltpu.make_async_copy(turner, table_in, load_sem.at[3]),
        pltpu.make_async_copy(qm, q_own, own_sem.at[0]),
    )

    @pl.when(live)
    def _():
        for load in loads:
            load.start()

    for via in sorted({via for via, _ in relay.values()}):

        @pl.when(me == via)
        def _():
            for row, m, p in slots:
                if relay[row, m][0] == via:
                    relay_copy(row, m, p).wait_recv()
                    relay_on(row, m, p).start()

    acc[...] = jnp.zeros_like(acc)
    acc_far[...] = jnp.zeros_like(acc_far)
    rows_i = lax.broadcasted_iota(jnp.int32, (block, block), 0)
    cols_i = lax.broadcasted_iota(jnp.int32, (block, block), 1)
    column = lax.broadcasted_iota(jnp.int32, (block, 1), 0)
    line = lax.broadcasted_iota(jnp.int32, (1, block), 1)

    @pl.when(live)
    def _():
        loads[0].wait()
        total = jnp.zeros((block, block), F32)
        for e in range(1, dist):
            factor = jnp.exp((line - (dist - e) * block).astype(F32) * beta)
            total = total + qb_in[e - 1] * factor
        row_sum[...] = jnp.broadcast_to(jnp.sum(total, axis=1, keepdims=True), row_sum.shape)
        loads[2].wait()
        loads[3].wait()
        first = jnp.sum(jnp.where(rows_i == cols_i, code_own[...].astype(F32), 0.0), axis=1, keepdims=True)
        table = jnp.exp(-table_in[...])
        entries = table.shape[1]
        table = jnp.concatenate([table, jnp.zeros((1, 128 - entries), F32)], axis=1)
        table = jnp.broadcast_to(table, (block, 128))
        loads[1].wait()
        code_send().wait_recv()
        both = first + code_in[...].astype(F32)
        allowed = jnp.where(jnp.logical_or(both == 3.0, both == 5.0), 1.0, 0.0)
        for start in range(0, block, 128):
            part = pl.ds(start, 128)
            found = jnp.take_along_axis(table, e_in[:, part], axis=1, mode="promise_in_bounds")
            weight[:, part] = found * allowed[:, start : start + 128]
        loads[4].wait()

    def column_sum(m, right, total):
        fade = jnp.exp((-(m + 1) * block - column).astype(F32) * beta)
        total[block : block + 1, :] += jnp.sum(right * fade, axis=0, keepdims=True)

    def listed(shifts):
        return sum(m * base**i for i, m in enumerate(shifts))

    if plan:
        far_list = jnp.int32(0)
        for device, shifts in plan.values():
            far_list = far_list + jnp.where(me == device, listed(shifts), 0)
        for c in range(CHUNKS):
            at = rows_of(c)
            if c < CHUNKS - 1:
                for count in sorted({len(shifts) for _, shifts in plan.values()}):

                    @pl.when(any_of(me, [device for device, shifts in plan.values() if len(shifts) == count]))
                    def _():
                        whole = (pl.ds(0, count), at)
                        remote(qm.at[whole], q_far.at[whole], q_send.at[0], q_recv.at[c], 0).wait_recv()

            def far_step(step, rest):
                m = rest % base - 1

                @pl.when(rest > 0)
                def _():
                    if c == 0:
                        r_copy(m + 1, 0).wait_recv()
                        right = r_in[m]
                        rf_h[m], rf_l[m] = split(right)
                        column_sum(m, right, acc_far)
                    if c == CHUNKS - 1:
                        here = (m, at)
                        slot = q_recv.at[CHUNKS - 1 + m]
                        remote(qm.at[here], q_far.at[here], q_send.at[0], slot, 0).wait_recv()
                    acc_far[at, :] += dot3(split(q_far[m, at, :]), (rf_h[m], rf_l[m]))

                return rest // base

            lax.fori_loop(0, dm, far_step, far_list)
            for row, (device, _) in plan.items():

                @pl.when(me == device)
                def _():
                    part_copy(c, row).start()

        for row, m in LATE:

            @pl.when(me == row + m)
            def _():
                relay_rest(row, m).start()

    own_list = jnp.int32(listed(range(1, dm + 1)))
    for row in range(live_rows) if plan else ():
        shifts = [m for m in order.get(row, range(1, dm + 1)) if home(row, m) == row]
        own_list = jnp.where(me == row, listed(shifts), own_list)
    own_list = jnp.where(live, own_list, 0)

    def own_step(step, rest):
        m = rest % base - 1

        @pl.when(rest > 0)
        def _():
            r_copy(m + 1, 0).wait_recv()
            right = r_in[m]
            column_sum(m, right, acc)
            acc[0:block, :] += dot3(split(q_own[m]), split(right))

        return rest // base

    lax.fori_loop(0, dm, own_step, own_list)

    if plan:

        @pl.when(any_of(me, list(plan)))
        def _():
            remote(acc_far, partial_in, part_sem.at[0], part_sem.at[1], 0).wait_recv()
            acc[...] += partial_in[...]

    sent = jnp.int32(0)
    for m in range(1, dist):
        row = me - m
        sent = sent + jnp.where(jnp.logical_and(row >= 0, row < live_rows), 1, 0)
    for row, (device, shifts) in plan.items():
        if device - row in shifts:
            sent = sent - jnp.where(me == device, 1, 0)
    for count in range(1, dist):

        @pl.when(sent == count)
        def _():
            whole = pl.ds(0, count)
            remote(qm1.at[whole], r_in.at[whole], r_send.at[0], r_recv.at[0], 0).wait_send()

    for row, (device, shifts) in plan.items():

        @pl.when(me == row)
        def _():
            whole = pl.ds(0, len(shifts))
            remote(qm.at[whole], q_far.at[whole], q_send.at[0], q_recv.at[0], 0).wait_send()

    @pl.when(me >= dist)
    def _():
        code_send().wait_send()

    if plan:

        @pl.when(any_of(me, [device for device, _ in plan.values()]))
        def _():
            remote(acc_far, partial_in, part_sem.at[0], part_sem.at[1], 0).wait_send()

    for via in sorted({via for via, _ in relay.values()}):

        @pl.when(me == via)
        def _():
            whole = pl.ds(0, sum(1 for key in slots if relay[key[:2]][0] == via))
            remote(relay_in.at[whole], relay_in.at[whole], relay_send.at[0], r_recv.at[0], 0).wait_send()


def finish(live_rows, dist, acc, weight, row_sum, pair_out, branch_out, multi_out):
    block = weight.shape[0]
    beta = 1.0 / (dist * block)
    live = lax.axis_index("row") < live_rows

    @pl.when(live)
    def _():
        column = lax.broadcasted_iota(jnp.int32, (block, 1), 0).astype(F32)
        line = lax.broadcasted_iota(jnp.int32, (1, block), 1).astype(F32)
        rows_i = lax.broadcasted_iota(jnp.int32, (block, block), 0)
        cols_i = lax.broadcasted_iota(jnp.int32, (block, block), 1)
        upper = jnp.where(cols_i >= rows_i, 1.0, 0.0).astype(BF16)
        summed = acc[0:block, :]
        pair = weight[...] * (1.0 + 0.8 * summed)
        pair_out[...] = pair
        high, low = split(pair * jnp.exp(line * beta))
        inner = mm(high, upper) + mm(low, upper)
        branch = (row_sum[:, 0:1] + inner) * (beta * jnp.exp(line * (-beta)))
        branch_out[...] = branch
        high, low = split(branch * jnp.exp(column * (-beta)))
        tails = acc[block : block + 1, :] + mm(upper, high) + mm(upper, low)
        multi_out[...] = summed + 0.01 * jnp.exp(column * beta) * tails

    @pl.when(jnp.logical_not(live))
    def _():
        for out in (pair_out, branch_out, multi_out):
            out[...] = jnp.zeros_like(out)


def solution(mesh):
    width = mesh.shape["row"]

    def per_device(qm, qm1, qb, codes, energy_index, turner):
        dm, block = qm.shape[2], qm.shape[3]
        dist = dm + 1
        known = width == 16 and dist == 8
        plan = PLAN if known else {}
        relay = RELAY if known else {}
        pieces = max([1] + [sum(n for v, n in relay.values() if v == via) for via, _ in relay.values()])
        blocks = pltpu.VMEM((dm, block, block), F32)
        halves = pltpu.VMEM((dm, block, block), BF16)
        square = jax.ShapeDtypeStruct((block, block), F32)
        tall = pltpu.VMEM((block + 8, block), F32)
        dma = pltpu.SemaphoreType.DMA
        anywhere = pl.BlockSpec(memory_space=pltpu.HBM)
        local = pl.BlockSpec(memory_space=pltpu.VMEM)
        middle = pl.pallas_call(
            functools.partial(kernel, plan, relay, ORDER if known else {}, width),
            out_shape=[
                pltpu.VMEM((block + 8, block), F32),
                pltpu.VMEM((block, block), F32),
                pltpu.VMEM((block, 128), F32),
            ],
            in_specs=[anywhere] * 6,
            out_specs=[local] * 3,
            scratch_shapes=[
                blocks, blocks, blocks, halves, halves, blocks,
                pltpu.VMEM((block, block), jnp.int32),
                pltpu.VMEM((1, block), jnp.int32),
                tall, tall, pltpu.VMEM((pieces, block // PIECES, block), F32),
                pltpu.VMEM((1, block), jnp.int32),
                pltpu.VMEM((1, turner.shape[0]), F32),
                dma((1,)), dma((1,)), dma((CHUNKS - 1 + dm,)), dma((1,)), dma((dm,)),
                dma((4,)), dma((2,)), dma((2,)), dma((1,)), dma((pieces,)),
            ],
            compiler_params=pltpu.CompilerParams(has_side_effects=True, collective_id=0),
        )(
            qm[0, 0], qm1[0, 0], qb[0, 0], energy_index[0, 0],
            codes[0], turner[None, :],
        )
        outs = pl.pallas_call(
            functools.partial(finish, width - dist, dist),
            out_shape=[square] * 3,
            in_specs=[local] * 3,
            out_specs=[local] * 3,
            compiler_params=pltpu.CompilerParams(vmem_limit_bytes=16 * 2**20),
        )(*middle)
        return tuple(out[None, None] for out in outs)

    return jax.shard_map(
        per_device,
        mesh=mesh,
        in_specs=(
            P("seq", "row", None, None, None),
            P("seq", "row", None, None, None),
            P("seq", "row", None, None, None),
            P("seq", "row", None),
            P("seq", "row", None, None),
            P(),
        ),
        out_specs=(
            P("seq", "row", None, None),
            P("seq", "row", None, None),
            P("seq", "row", None, None),
        ),
        check_vma=False,
    )
```

time: 33.8 us -> 31.4 us (0.929)
  the two profiles are of different devices: /device:TPU:8 before, /device:TPU:12 now
where the time goes in v3:
time: 31.4 us; the launch traced here: 31.3 us
  Pallas kernels  30.6 us (97%)
  between operations  0.64 us (2%)
    pallas_call x1, Pallas kernels, per_device(): pl.pallas_call(functools.partial(kernel, plan, relay, ORDER if known else...  29.2 us
    pallas_call x1, Pallas kernels, per_device(): pl.pallas_call(functools.partial(finish, width - dist, dist), out_shape=[...  1.44 us

profile of v3, /device:TPU:12, one launch (start us, length us, event | category | flops | bytes accessed | tf_op | source)
XLA Modules:
  0.0 31.3 jit_solution(12065298334356313141)
XLA Ops:
  0.6 29.2 %shard_map.85 = (f32[264,256]{1,0:T(8,128)S(1)}, f32[256,256]{1,0:T(8,128)S(1)}, f32[256,128]{1,0:T(8,128)S(1)}) custom-call(f32[7,256,256]{2,1,0:T(8,128)} %bitcast.9, f32[7,256,256]{2,1,0:T(8,128)} %bitcast.10, f32[7,256,256]{2,1,0:T(8,128)} %bitcast.11, s32[256,256]{1,0:T(8,128)} %bitcast.12, s32[1,256]{1,0:T(1,128)} %bitcast.13, f32[1,64]{1,0:T(1,128)} %bitcast.14), custom_call_target="tpu_custom_call" | custom-call | tf_op jit(solution)/shard_map/pallas_call | solution.py:428
  29.8 1.4 %shard_map.86 = (f32[256,256]{1,0:T(8,128)}, f32[256,256]{1,0:T(8,128)}, f32[256,256]{1,0:T(8,128)}) custom-call(f32[264,256]{1,0:T(8,128)S(1)} %get-tuple-element.9.acc, f32[256,256]{1,0:T(8,128)S(1)} %get-tuple-element.10.weight, f32[256,128]{1,0:T(8,128)S(1)} %get-tuple-element.11.row_sum), custom_call_target="tpu_custom_call" | custom-call | tf_op jit(solution)/shard_map/pallas_call | solution.py:452

commit v4 on v3

--- a/solution.py
+++ b/solution.py
@@ -12,23 +12,29 @@
 
 PLAN = {
     1: (5, (4, 3, 6, 5, 7)),
-    3: (7, (4, 3, 1, 2, 6, 5, 7)),
+    3: (6, (3, 1, 2, 7, 6, 5)),
     4: (8, (7, 6)),
     5: (9, (4, 3, 6, 5, 7)),
-    7: (11, (4, 3, 7, 5, 6, 2, 1)),
+    7: (11, (4, 3, 7, 1, 2, 5, 6)),
 }
 RELAY = {
-    (6, 7): (15, 2),
-    (6, 6): (14, 2),
-    (2, 7): (10, 2),
-    (6, 3): (10, 2),
-    (6, 2): (10, 1),
+    (6, 7): (15, 4, 0),
+    (6, 6): (14, 4, 0),
+    (2, 6): (10, 4, 0),
+    (6, 2): (10, 2, 4),
+    (6, 3): (10, 4, 0),
+    (7, 5): (14, 4, 1),
+    (7, 6): (15, 4, 1),
 }
-LATE = ((6, 2),)
-ORDER = {6: (1, 5, 4, 7, 6, 3, 2)}
+HELD = (
+    {8: (10, 11), 9: (10, 11)},
+    {4: (2, 6), 5: (2, 6), 8: (2, 6), 9: (2, 6)},
+)
+ORDER = {6: (1, 7, 6, 5, 4, 3, 2)}
 SHARES = (4, 2, 1, 1)
 CHUNKS = len(SHARES)
-PIECES = 2
+PIECES = 4
+HEAD = 8
 
 
 def split(x):
@@ -54,9 +60,9 @@
 
 
 def kernel(
-    plan, relay, order, width, qm, qm1, qb, eidx, codes, turner, acc, weight, row_sum,
-    q_own, r_in, q_far, rf_h, rf_l, qb_in, e_in, code_in, acc_far, partial_in, relay_in, code_own, table_in,
-    own_sem, q_send, q_recv, r_send, r_recv, load_sem, code_sem, part_sem, relay_send, relay_recv,
+    plan, relay, width, qm, qm1, qb, eidx, codes, turner, acc, weight, row_sum,
+    q_own, r_in, r_far, q_far, rf_h, rf_l, qb_in, e_in, code_in, acc_far, partial_in, relay_in, code_own, table_in,
+    own_sem, q_send, q_recv, r_send, r_recv, rf_recv, load_sem, code_sem, part_sem, held_sem,
 ):
     dm, block = qm.shape[0], qm.shape[1]
     dist = dm + 1
@@ -65,6 +71,7 @@
     base = dm + 1
     me = lax.axis_index("row")
     live = me < live_rows
+    relay_send, relay_recv = q_send, q_recv
     unit = block // sum(SHARES)
     piece = block // PIECES
 
@@ -74,24 +81,56 @@
             device_id={"row": device}, device_id_type=pl.DeviceIdType.MESH,
         )
 
+    def near(row):
+        return jnp.logical_and(row >= 0, row < live_rows)
+
     def home(row, m):
         device, shifts = plan.get(row, (None, ()))
         return device if m in shifts else row
 
+    held = HELD if plan else ()
+    order = ORDER if plan else {}
+    waiting = []
+    for group in held:
+        lists = {source: [] for source in group}
+        for source in group:
+            for row in range(min(live_rows, source) - 1, max(source - dist, -1), -1):
+                m = source - row
+                via, count, _ = relay.get((row, m), (None, 0, 0))
+                if home(row, m) in group[source] and count < PIECES:
+                    lists[source].append((row, m, False))
+                if via in group[source]:
+                    lists[source].append((row, m, True))
+            lists[source].sort(key=lambda item: (item[2], item[0] not in (3, 7), -item[0]))
+        waiting.append(lists)
+    rests = {(row, m) for lists in waiting for keys in lists.values() for row, m, part in keys if not part}
+    parts = {(row, m) for lists in waiting for keys in lists.values() for row, m, part in keys if part}
+
     def apart(m):
-        return [row for row in range(live_rows) if (row, m) in relay or home(row, m) != row] if plan else []
+        if not plan:
+            return []
+        return [
+            row for row in range(live_rows)
+            if (row, m) in relay or (row, m) in rests or home(row, m) != row
+        ]
+
+    def held_send(row, m):
+        if (row, m) in relay:
+            relay_rest(row, m).start()
+        else:
+            (r_copy if home(row, m) == row else rf_copy)(m, home(row, m)).start()
 
     def direct(m):
         row = me - m
-        ok = jnp.logical_and(row >= 0, row < live_rows)
+        ok = near(row)
         rows = apart(m)
         return jnp.logical_and(ok, jnp.logical_not(any_of(row, rows))) if rows else ok
 
     def code_send():
         return remote(codes, code_in, code_sem.at[0], code_sem.at[1], me - dist)
 
-    def rows_of(c, more=0):
-        return pl.ds(sum(SHARES[:c]) * unit, SHARES[c] * unit + more)
+    def rows_of(c, shift=0):
+        return pl.ds(sum(SHARES[:c]) * unit + shift, SHARES[c] * unit)
 
     def q_copy(m, c, device):
         at = (m - 1, rows_of(c))
@@ -101,10 +140,16 @@
     def r_copy(m, device):
         return remote(qm1.at[dm - m], r_in.at[m - 1], r_send.at[0], r_recv.at[m - 1], device)
 
+    def rf_copy(m, device):
+        return remote(qm1.at[dm - m], r_far.at[m - 1], r_send.at[0], rf_recv.at[m - 1], device)
+
+    def right_at(row, m):
+        return (r_in, r_recv) if home(row, m) == row else (r_far, rf_recv)
+
+    turns = sorted((rank + p, row, m, p) for (row, m), (_, count, rank) in relay.items() for p in range(count))
     slots = {}
-    for (row, m), (via, count) in relay.items():
-        for p in range(count):
-            slots[row, m, p] = sum(1 for key in slots if relay[key[:2]][0] == via)
+    for _, row, m, p in turns:
+        slots[row, m, p] = sum(1 for key in slots if relay[key[:2]][0] == relay[row, m][0])
 
     def relay_copy(row, m, p):
         slot = slots[row, m, p]
@@ -115,20 +160,20 @@
 
     def relay_on(row, m, p):
         at = pl.ds(p * piece, piece)
+        into, sem = right_at(row, m)
         return remote(
-            relay_in.at[slots[row, m, p]], r_in.at[m - 1, at],
-            relay_send.at[0], r_recv.at[m - 1], home(row, m),
+            relay_in.at[slots[row, m, p]], into.at[m - 1, at], relay_send.at[0], sem.at[m - 1], home(row, m)
         )
 
     def relay_rest(row, m):
         start = relay[row, m][1] * piece
         at = pl.ds(start, block - start)
-        return remote(
-            qm1.at[dm - m, at], r_in.at[m - 1, at], r_send.at[0], r_recv.at[m - 1], home(row, m)
-        )
+        into, sem = right_at(row, m)
+        return remote(qm1.at[dm - m, at], into.at[m - 1, at], r_send.at[0], sem.at[m - 1], home(row, m))
 
     def part_copy(c, device):
-        at = rows_of(c, 8 if c == CHUNKS - 1 else 0)
+        start = HEAD + sum(SHARES[:c]) * unit if c else 0
+        at = pl.ds(start, HEAD + sum(SHARES[: c + 1]) * unit - start)
         return remote(acc_far.at[at], partial_in.at[at], part_sem.at[0], part_sem.at[1], device)
 
     barrier = pltpu.get_barrier_semaphore()
@@ -138,35 +183,58 @@
             barrier, inc=1, device_id={"row": device}, device_id_type=pl.DeviceIdType.MESH
         )
 
-    extra = set()
-    for row, (device, shifts) in plan.items():
-        extra |= {(row, device), (device, row)} | {(row + m, device) for m in shifts}
-    for (row, m), (via, _) in relay.items():
-        extra |= {(row + m, via), (via, home(row, m))}
-    extra = sorted((s, d) for s, d in extra if s != d and not (d < live_rows and 1 <= s - d <= dist))
-
-    @pl.when(live)
-    def _():
+    if plan:
+        pairs = {(device, device - dist) for device in range(dist, width)}
+        for row in range(live_rows):
+            for m in range(1, dist):
+                source, device = row + m, home(row, m)
+                via, count, _ = relay.get((row, m), (None, 0, 0))
+                if count:
+                    pairs |= {(source, via), (via, device)}
+                if count < PIECES:
+                    pairs.add((source, device))
+        for row, (device, _) in plan.items():
+            pairs |= {(row, device), (device, row)}
+        for group in held:
+            for source, devices in group.items():
+                pairs -= {(source, device) for device in devices}
+                pairs |= {(device, source) for device in devices}
+        pairs = sorted((s, d) for s, d in pairs if s != d)
+        awaited = jnp.int32(0)
+        for device in range(width):
+            sources = [s for s, d in pairs if d == device]
+            awaited = awaited + jnp.where(me == device, sum(1 for s, _ in pairs if s == device), 0)
+            if sources:
+
+                @pl.when(me == device)
+                def _():
+                    for source in sources:
+                        greet(source)
+
+    else:
+
+        @pl.when(live)
+        def _():
+            for m in range(1, dist + 1):
+                greet(me + m)
+
+        awaited = jnp.int32(0)
         for m in range(1, dist + 1):
-            greet(me + m)
-
-    for device in sorted({d for _, d in extra}):
-
-        @pl.when(me == device)
-        def _():
-            for source in [s for s, d in extra if d == device]:
-                greet(source)
-
-    awaited = jnp.int32(0)
-    for m in range(1, dist + 1):
-        row = me - m
-        awaited = awaited + jnp.where(jnp.logical_and(row >= 0, row < live_rows), 1, 0)
-    for source in sorted({s for s, _ in extra}):
-        awaited = awaited + jnp.where(me == source, sum(1 for s, _ in extra if s == source), 0)
+            awaited = awaited + jnp.where(near(me - m), 1, 0)
 
     @pl.when(awaited > 0)
     def _():
         pl.semaphore_wait(barrier, awaited)
+
+    for n, group in enumerate(held):
+        for device in sorted({device for devices in group.values() for device in devices}):
+
+            @pl.when(me == device)
+            def _():
+                for source in [source for source, devices in group.items() if device in devices]:
+                    pl.semaphore_signal(
+                        held_sem.at[n], inc=1, device_id={"row": source}, device_id_type=pl.DeviceIdType.MESH
+                    )
 
     @pl.when(me >= dist)
     def _():
@@ -174,15 +242,15 @@
 
     for m in range(dm, 0, -1):
         for row, (device, shifts) in plan.items():
-            if m not in shifts or (row, m) in relay:
+            if m not in shifts or (row, m) in relay or (row, m) in rests:
                 continue
 
             @pl.when(me == row + m)
             def _():
                 if row + m == device:
-                    pltpu.make_async_copy(qm1.at[dm - m], r_in.at[m - 1], r_recv.at[m - 1]).start()
+                    pltpu.make_async_copy(qm1.at[dm - m], r_far.at[m - 1], rf_recv.at[m - 1]).start()
                 else:
-                    r_copy(m, device).start()
+                    rf_copy(m, device).start()
 
     for row, (device, shifts) in plan.items():
 
@@ -192,14 +260,16 @@
                 for m in shifts:
                     q_copy(m, c, device).start()
 
-    for (row, m), (via, count) in relay.items():
-
-        @pl.when(me == row + m)
-        def _():
-            for p in range(count):
-                relay_copy(row, m, p).start()
-            if count < PIECES and (row, m) not in LATE:
-                relay_rest(row, m).start()
+    for source in sorted({row + m for row, m in relay}):
+
+        @pl.when(me == source)
+        def _():
+            for row, m, p in slots:
+                if row + m == source and (row, m) not in parts:
+                    relay_copy(row, m, p).start()
+            for (row, m), (_, count, _) in relay.items():
+                if row + m == source and count < PIECES and (row, m) not in rests:
+                    relay_rest(row, m).start()
 
     for m in range(dm, 0, -1):
 
@@ -220,7 +290,7 @@
         for load in loads:
             load.start()
 
-    for via in sorted({via for via, _ in relay.values()}):
+    for via in sorted({via for via, _, _ in relay.values()}):
 
         @pl.when(me == via)
         def _():
@@ -261,12 +331,43 @@
             weight[:, part] = found * allowed[:, start : start + 128]
         loads[4].wait()
 
+    for n, lists in enumerate(waiting):
+        for source, keys in lists.items():
+
+            @pl.when(me == source)
+            def _():
+                pl.semaphore_wait(held_sem.at[n], len(held[n][source]))
+                for row, m, part in keys:
+                    if part:
+                        for p in range(relay[row, m][1]):
+                            relay_copy(row, m, p).start()
+                    else:
+                        held_send(row, m)
+
     def column_sum(m, right, total):
         fade = jnp.exp((-(m + 1) * block - column).astype(F32) * beta)
-        total[block : block + 1, :] += jnp.sum(right * fade, axis=0, keepdims=True)
+        total[0:1, :] += jnp.sum(right * fade, axis=0, keepdims=True)
 
     def listed(shifts):
         return sum(m * base**i for i, m in enumerate(shifts))
+
+    own_list = jnp.int32(listed(range(1, dm + 1)))
+    for row in range(live_rows) if plan else ():
+        shifts = [m for m in order.get(row, range(1, dm + 1)) if home(row, m) == row]
+        own_list = jnp.where(me == row, listed(shifts), own_list)
+    own_list = jnp.where(live, own_list, 0)
+
+    def own_step(step, rest):
+        m = rest % base - 1
+
+        @pl.when(rest > 0)
+        def _():
+            r_copy(m + 1, 0).wait_recv()
+            right = r_in[m]
+            column_sum(m, right, acc)
+            acc[HEAD:, :] += dot3(split(q_own[m]), split(right))
+
+        return rest // base
 
     if plan:
         far_list = jnp.int32(0)
@@ -288,15 +389,15 @@
                 @pl.when(rest > 0)
                 def _():
                     if c == 0:
-                        r_copy(m + 1, 0).wait_recv()
-                        right = r_in[m]
+                        rf_copy(m + 1, 0).wait_recv()
+                        right = r_far[m]
                         rf_h[m], rf_l[m] = split(right)
                         column_sum(m, right, acc_far)
                     if c == CHUNKS - 1:
                         here = (m, at)
                         slot = q_recv.at[CHUNKS - 1 + m]
                         remote(qm.at[here], q_far.at[here], q_send.at[0], slot, 0).wait_recv()
-                    acc_far[at, :] += dot3(split(q_far[m, at, :]), (rf_h[m], rf_l[m]))
+                    acc_far[rows_of(c, HEAD), :] += dot3(split(q_far[m, at, :]), (rf_h[m], rf_l[m]))
 
                 return rest // base
 
@@ -307,30 +408,6 @@
                 def _():
                     part_copy(c, row).start()
 
-        for row, m in LATE:
-
-            @pl.when(me == row + m)
-            def _():
-                relay_rest(row, m).start()
-
-    own_list = jnp.int32(listed(range(1, dm + 1)))
-    for row in range(live_rows) if plan else ():
-        shifts = [m for m in order.get(row, range(1, dm + 1)) if home(row, m) == row]
-        own_list = jnp.where(me == row, listed(shifts), own_list)
-    own_list = jnp.where(live, own_list, 0)
-
-    def own_step(step, rest):
-        m = rest % base - 1
-
-        @pl.when(rest > 0)
-        def _():
-            r_copy(m + 1, 0).wait_recv()
-            right = r_in[m]
-            column_sum(m, right, acc)
-            acc[0:block, :] += dot3(split(q_own[m]), split(right))
-
-        return rest // base
-
     lax.fori_loop(0, dm, own_step, own_list)
 
     if plan:
@@ -342,8 +419,7 @@
 
     sent = jnp.int32(0)
     for m in range(1, dist):
-        row = me - m
-        sent = sent + jnp.where(jnp.logical_and(row >= 0, row < live_rows), 1, 0)
+        sent = sent + jnp.where(near(me - m), 1, 0)
     for row, (device, shifts) in plan.items():
         if device - row in shifts:
             sent = sent - jnp.where(me == device, 1, 0)
@@ -371,7 +447,7 @@
         def _():
             remote(acc_far, partial_in, part_sem.at[0], part_sem.at[1], 0).wait_send()
 
-    for via in sorted({via for via, _ in relay.values()}):
+    for via in sorted({via for via, _, _ in relay.values()}):
 
         @pl.when(me == via)
         def _():
@@ -391,7 +467,7 @@
         rows_i = lax.broadcasted_iota(jnp.int32, (block, block), 0)
         cols_i = lax.broadcasted_iota(jnp.int32, (block, block), 1)
         upper = jnp.where(cols_i >= rows_i, 1.0, 0.0).astype(BF16)
-        summed = acc[0:block, :]
+        summed = acc[HEAD:, :]
         pair = weight[...] * (1.0 + 0.8 * summed)
         pair_out[...] = pair
         high, low = split(pair * jnp.exp(line * beta))
@@ -399,7 +475,7 @@
         branch = (row_sum[:, 0:1] + inner) * (beta * jnp.exp(line * (-beta)))
         branch_out[...] = branch
         high, low = split(branch * jnp.exp(column * (-beta)))
-        tails = acc[block : block + 1, :] + mm(upper, high) + mm(upper, low)
+        tails = acc[0:1, :] + mm(upper, high) + mm(upper, low)
         multi_out[...] = summed + 0.01 * jnp.exp(column * beta) * tails
 
     @pl.when(jnp.logical_not(live))
@@ -417,32 +493,33 @@
         known = width == 16 and dist == 8
         plan = PLAN if known else {}
         relay = RELAY if known else {}
-        pieces = max([1] + [sum(n for v, n in relay.values() if v == via) for via, _ in relay.values()])
+        pieces = max([1] + [sum(n for v, n, _ in relay.values() if v == via) for via, _, _ in relay.values()])
         blocks = pltpu.VMEM((dm, block, block), F32)
         halves = pltpu.VMEM((dm, block, block), BF16)
         square = jax.ShapeDtypeStruct((block, block), F32)
-        tall = pltpu.VMEM((block + 8, block), F32)
+        tall = pltpu.VMEM((block + HEAD, block), F32)
         dma = pltpu.SemaphoreType.DMA
         anywhere = pl.BlockSpec(memory_space=pltpu.HBM)
         local = pl.BlockSpec(memory_space=pltpu.VMEM)
         middle = pl.pallas_call(
-            functools.partial(kernel, plan, relay, ORDER if known else {}, width),
+            functools.partial(kernel, plan, relay, width),
             out_shape=[
-                pltpu.VMEM((block + 8, block), F32),
+                pltpu.VMEM((block + HEAD, block), F32),
                 pltpu.VMEM((block, block), F32),
                 pltpu.VMEM((block, 128), F32),
             ],
             in_specs=[anywhere] * 6,
             out_specs=[local] * 3,
             scratch_shapes=[
-                blocks, blocks, blocks, halves, halves, blocks,
+                blocks, blocks, blocks, blocks, halves, halves, blocks,
                 pltpu.VMEM((block, block), jnp.int32),
                 pltpu.VMEM((1, block), jnp.int32),
                 tall, tall, pltpu.VMEM((pieces, block // PIECES, block), F32),
                 pltpu.VMEM((1, block), jnp.int32),
                 pltpu.VMEM((1, turner.shape[0]), F32),
-                dma((1,)), dma((1,)), dma((CHUNKS - 1 + dm,)), dma((1,)), dma((dm,)),
-                dma((4,)), dma((2,)), dma((2,)), dma((1,)), dma((pieces,)),
+                dma((1,)), dma((1,)), dma((CHUNKS - 1 + dm,)), dma((1,)), dma((dm,)), dma((dm,)),
+                dma((4,)), dma((2,)), dma((2,)),
+                pltpu.SemaphoreType.REGULAR((len(HELD),)),
             ],
             compiler_params=pltpu.CompilerParams(has_side_effects=True, collective_id=0),
         )(

time: 31.4 us -> 30.7 us (0.978)
  the two profiles are of different devices: /device:TPU:12 before, /device:TPU:5 now
where the time goes in v4:
time: 30.7 us; the launch traced here: 30.6 us
  Pallas kernels  29.9 us (97%)
  between operations  0.64 us (2%)
    pallas_call x1, Pallas kernels, per_device(): pl.pallas_call(functools.partial(kernel, plan, relay, width), out_shape=[...  28.5 us
    pallas_call x1, Pallas kernels, per_device(): pl.pallas_call(functools.partial(finish, width - dist, dist), out_shape=[...  1.44 us

profile of v4, /device:TPU:5, one launch (start us, length us, event | category | flops | bytes accessed | tf_op | source)
XLA Modules:
  0.0 30.6 jit_solution(594520463744386001)
XLA Ops:
  0.6 28.5 %shard_map.85 = (f32[264,256]{1,0:T(8,128)S(1)}, f32[256,256]{1,0:T(8,128)S(1)}, f32[256,128]{1,0:T(8,128)S(1)}) custom-call(f32[7,256,256]{2,1,0:T(8,128)} %bitcast.9, f32[7,256,256]{2,1,0:T(8,128)} %bitcast.10, f32[7,256,256]{2,1,0:T(8,128)} %bitcast.11, s32[256,256]{1,0:T(8,128)} %bitcast.12, s32[1,256]{1,0:T(1,128)} %bitcast.13, f32[1,64]{1,0:T(1,128)} %bitcast.14), custom_call_target="tpu_custom_call" | custom-call | tf_op jit(solution)/shard_map/pallas_call | solution.py:504
  29.2 1.4 %shard_map.86 = (f32[256,256]{1,0:T(8,128)}, f32[256,256]{1,0:T(8,128)}, f32[256,256]{1,0:T(8,128)}) custom-call(f32[264,256]{1,0:T(8,128)S(1)} %get-tuple-element.9.acc, f32[256,256]{1,0:T(8,128)S(1)} %get-tuple-element.10.weight, f32[256,128]{1,0:T(8,128)S(1)} %get-tuple-element.11.row_sum), custom_call_target="tpu_custom_call" | custom-call | tf_op jit(solution)/shard_map/pallas_call | solution.py:529

commit v5 on v4

--- a/solution.py
+++ b/solution.py
@@ -27,9 +27,10 @@
     (7, 6): (15, 4, 1),
 }
 HELD = (
-    {8: (10, 11), 9: (10, 11)},
-    {4: (2, 6), 5: (2, 6), 8: (2, 6), 9: (2, 6)},
+    {4: (6,), 5: (6,), 8: (10, 11), 9: (10, 11)},
+    {4: (2,), 5: (2,), 8: (2, 6), 9: (2, 6)},
 )
+DEFER = {8: ((4, 4),)}
 ORDER = {6: (1, 7, 6, 5, 4, 3, 2)}
 SHARES = (4, 2, 1, 1)
 CHUNKS = len(SHARES)
@@ -90,6 +91,7 @@
 
     held = HELD if plan else ()
     order = ORDER if plan else {}
+    defer = DEFER if plan else {}
     waiting = []
     for group in held:
         lists = {source: [] for source in group}
@@ -103,6 +105,8 @@
                     lists[source].append((row, m, True))
             lists[source].sort(key=lambda item: (item[2], item[0] not in (3, 7), -item[0]))
         waiting.append(lists)
+    for source, keys in defer.items():
+        waiting[-1][source] += [(row, m, False) for row, m in keys]
     rests = {(row, m) for lists in waiting for keys in lists.values() for row, m, part in keys if not part}
     parts = {(row, m) for lists in waiting for keys in lists.values() for row, m, part in keys if part}
 
@@ -170,6 +174,19 @@
         at = pl.ds(start, block - start)
         into, sem = right_at(row, m)
         return remote(qm1.at[dm - m, at], into.at[m - 1, at], r_send.at[0], sem.at[m - 1], home(row, m))
+
+    def send_held(n):
+        for source, keys in waiting[n].items():
+
+            @pl.when(me == source)
+            def _():
+                pl.semaphore_wait(held_sem.at[n], len(held[n][source]))
+                for row, m, part in keys:
+                    if part:
+                        for p in range(relay[row, m][1]):
+                            relay_copy(row, m, p).start()
+                    else:
+                        held_send(row, m)
 
     def part_copy(c, device):
         start = HEAD + sum(SHARES[:c]) * unit if c else 0
@@ -290,6 +307,9 @@
         for load in loads:
             load.start()
 
+    if held:
+        send_held(0)
+
     for via in sorted({via for via, _, _ in relay.values()}):
 
         @pl.when(me == via)
@@ -331,18 +351,8 @@
             weight[:, part] = found * allowed[:, start : start + 128]
         loads[4].wait()
 
-    for n, lists in enumerate(waiting):
-        for source, keys in lists.items():
-
-            @pl.when(me == source)
-            def _():
-                pl.semaphore_wait(held_sem.at[n], len(held[n][source]))
-                for row, m, part in keys:
-                    if part:
-                        for p in range(relay[row, m][1]):
-                            relay_copy(row, m, p).start()
-                    else:
-                        held_send(row, m)
+    for n in range(1, len(held)):
+        send_held(n)
 
     def column_sum(m, right, total):
         fade = jnp.exp((-(m + 1) * block - column).astype(F32) * beta)

time: 30.7 us -> 30.4 us (level)
  the two profiles are of different devices: /device:TPU:5 before, /device:TPU:8 now
where the time goes in v5:
time: 30.4 us; the launch traced here: 29.9 us
  Pallas kernels  29.3 us (96%)
  between operations  0.64 us (2%)
    pallas_call x1, Pallas kernels, per_device(): pl.pallas_call(functools.partial(kernel, plan, relay, width), out_shape=[...  27.8 us
    pallas_call x1, Pallas kernels, per_device(): pl.pallas_call(functools.partial(finish, width - dist, dist), out_shape=[...  1.44 us

profile of v5, /device:TPU:8, one launch (start us, length us, event | category | flops | bytes accessed | tf_op | source)
XLA Modules:
  0.0 29.9 jit_solution(5549093204625940186)
XLA Ops:
  0.6 27.8 %shard_map.85 = (f32[264,256]{1,0:T(8,128)S(1)}, f32[256,256]{1,0:T(8,128)S(1)}, f32[256,128]{1,0:T(8,128)S(1)}) custom-call(f32[7,256,256]{2,1,0:T(8,128)} %bitcast.9, f32[7,256,256]{2,1,0:T(8,128)} %bitcast.10, f32[7,256,256]{2,1,0:T(8,128)} %bitcast.11, s32[256,256]{1,0:T(8,128)} %bitcast.12, s32[1,256]{1,0:T(1,128)} %bitcast.13, f32[1,64]{1,0:T(1,128)} %bitcast.14), custom_call_target="tpu_custom_call" | custom-call | tf_op jit(solution)/shard_map/pallas_call | solution.py:514
  28.5 1.4 %shard_map.86 = (f32[256,256]{1,0:T(8,128)}, f32[256,256]{1,0:T(8,128)}, f32[256,256]{1,0:T(8,128)}) custom-call(f32[264,256]{1,0:T(8,128)S(1)} %get-tuple-element.9.acc, f32[256,256]{1,0:T(8,128)S(1)} %get-tuple-element.10.weight, f32[256,128]{1,0:T(8,128)S(1)} %get-tuple-element.11.row_sum), custom_call_target="tpu_custom_call" | custom-call | tf_op jit(solution)/shard_map/pallas_call | solution.py:539

commit v6 on v5

--- a/solution.py
+++ b/solution.py
@@ -13,15 +13,15 @@
 PLAN = {
     1: (5, (4, 3, 6, 5, 7)),
     3: (6, (3, 1, 2, 7, 6, 5)),
-    4: (8, (7, 6)),
-    5: (9, (4, 3, 6, 5, 7)),
+    4: (8, (4, 5, 7, 6)),
+    5: (9, (3, 6, 5, 7)),
     7: (11, (4, 3, 7, 1, 2, 5, 6)),
 }
 RELAY = {
     (6, 7): (15, 4, 0),
     (6, 6): (14, 4, 0),
     (2, 6): (10, 4, 0),
-    (6, 2): (10, 2, 4),
+    (6, 2): (10, 1, 4),
     (6, 3): (10, 4, 0),
     (7, 5): (14, 4, 1),
     (7, 6): (15, 4, 1),
@@ -30,7 +30,7 @@
     {4: (6,), 5: (6,), 8: (10, 11), 9: (10, 11)},
     {4: (2,), 5: (2,), 8: (2, 6), 9: (2, 6)},
 )
-DEFER = {8: ((4, 4),)}
+SPLIT = ((5, 3),)
 ORDER = {6: (1, 7, 6, 5, 4, 3, 2)}
 SHARES = (4, 2, 1, 1)
 CHUNKS = len(SHARES)
@@ -63,7 +63,7 @@
 def kernel(
     plan, relay, width, qm, qm1, qb, eidx, codes, turner, acc, weight, row_sum,
     q_own, r_in, r_far, q_far, rf_h, rf_l, qb_in, e_in, code_in, acc_far, partial_in, relay_in, code_own, table_in,
-    own_sem, q_send, q_recv, r_send, r_recv, rf_recv, load_sem, code_sem, part_sem, held_sem,
+    own_sem, q_send, q_recv, r_send, r_recv, rf_recv, load_sem, code_sem, part_sem, held_sem, half_sem,
 ):
     dm, block = qm.shape[0], qm.shape[1]
     dist = dm + 1
@@ -91,7 +91,8 @@
 
     held = HELD if plan else ()
     order = ORDER if plan else {}
-    defer = DEFER if plan else {}
+    halved = SPLIT if plan else ()
+    half = block // 2
     waiting = []
     for group in held:
         lists = {source: [] for source in group}
@@ -100,15 +101,16 @@
                 m = source - row
                 via, count, _ = relay.get((row, m), (None, 0, 0))
                 if home(row, m) in group[source] and count < PIECES:
-                    lists[source].append((row, m, False))
+                    lists[source].append((row, m, "rest"))
                 if via in group[source]:
-                    lists[source].append((row, m, True))
-            lists[source].sort(key=lambda item: (item[2], item[0] not in (3, 7), -item[0]))
+                    lists[source].append((row, m, "relay"))
+            lists[source].sort(key=lambda item: (item[2] == "relay", item[0] not in (3, 7), -item[0]))
         waiting.append(lists)
-    for source, keys in defer.items():
-        waiting[-1][source] += [(row, m, False) for row, m in keys]
-    rests = {(row, m) for lists in waiting for keys in lists.values() for row, m, part in keys if not part}
-    parts = {(row, m) for lists in waiting for keys in lists.values() for row, m, part in keys if part}
+    for row, m in halved:
+        waiting[-1][row + m].insert(1, (row, m, "half"))
+    kinds = [item for lists in waiting for keys in lists.values() for item in keys]
+    rests = {(row, m) for row, m, kind in kinds if kind == "rest"}
+    parts = {(row, m) for row, m, kind in kinds if kind == "relay"}
 
     def apart(m):
         if not plan:
@@ -136,8 +138,8 @@
     def rows_of(c, shift=0):
         return pl.ds(sum(SHARES[:c]) * unit + shift, SHARES[c] * unit)
 
-    def q_copy(m, c, device):
-        at = (m - 1, rows_of(c))
+    def q_copy(row, m, c, device):
+        at = (m - 1, rows_of(c), pl.ds(0, half if (row, m) in halved else block))
         slot = c if c < CHUNKS - 1 else CHUNKS - 2 + m
         return remote(qm.at[at], q_far.at[at], q_send.at[0], q_recv.at[slot], device)
 
@@ -146,6 +148,21 @@
 
     def rf_copy(m, device):
         return remote(qm1.at[dm - m], r_far.at[m - 1], r_send.at[0], rf_recv.at[m - 1], device)
+
+    def half_copy(m, device):
+        at = pl.ds(half, block - half)
+        return remote(qm1.at[dm - m, at], r_in.at[m - 1, at], half_sem.at[0], r_recv.at[m - 1], device)
+
+    def units(row):
+        shifts = plan[row][1]
+        return 2 * len(shifts) - sum(1 for m in shifts if (row, m) in halved)
+
+    def q_units(count, rows):
+        if count % 2 == 0:
+            at = (pl.ds(0, count // 2), rows)
+        else:
+            at = (pl.ds(0, count), rows, pl.ds(0, half))
+        return at
 
     def right_at(row, m):
         return (r_in, r_recv) if home(row, m) == row else (r_far, rf_recv)
@@ -181,10 +198,12 @@
             @pl.when(me == source)
             def _():
                 pl.semaphore_wait(held_sem.at[n], len(held[n][source]))
-                for row, m, part in keys:
-                    if part:
+                for row, m, kind in keys:
+                    if kind == "relay":
                         for p in range(relay[row, m][1]):
                             relay_copy(row, m, p).start()
+                    elif kind == "half":
+                        half_copy(m, row).start()
                     else:
                         held_send(row, m)
 
@@ -210,6 +229,8 @@
                     pairs |= {(source, via), (via, device)}
                 if count < PIECES:
                     pairs.add((source, device))
+                if (row, m) in halved:
+                    pairs.add((source, row))
         for row, (device, _) in plan.items():
             pairs |= {(row, device), (device, row)}
         for group in held:
@@ -275,7 +296,7 @@
         def _():
             for c in range(CHUNKS):
                 for m in shifts:
-                    q_copy(m, c, device).start()
+                    q_copy(row, m, c, device).start()
 
     for source in sorted({row + m for row, m in relay}):
 
@@ -321,6 +342,21 @@
 
     acc[...] = jnp.zeros_like(acc)
     acc_far[...] = jnp.zeros_like(acc_far)
+    for row, m in halved:
+
+        @pl.when(me == plan[row][0])
+        def _():
+            q_far[m - 1, :, half:] = jnp.zeros((block, block - half), F32)
+
+        @pl.when(me == row)
+        def _():
+            r_in[m - 1, 0:half, :] = jnp.zeros((half, block), F32)
+
+    @pl.when(jnp.logical_not(live))
+    def _():
+        weight[...] = jnp.zeros_like(weight)
+        row_sum[...] = jnp.zeros_like(row_sum)
+
     rows_i = lax.broadcasted_iota(jnp.int32, (block, block), 0)
     cols_i = lax.broadcasted_iota(jnp.int32, (block, block), 1)
     column = lax.broadcasted_iota(jnp.int32, (block, 1), 0)
@@ -358,12 +394,18 @@
         fade = jnp.exp((-(m + 1) * block - column).astype(F32) * beta)
         total[0:1, :] += jnp.sum(right * fade, axis=0, keepdims=True)
 
+    def is_half(m, place):
+        hit = jnp.bool_(False)
+        for row, shift in halved:
+            hit = jnp.logical_or(hit, jnp.logical_and(me == place(row, shift), m == shift - 1))
+        return hit
+
     def listed(shifts):
         return sum(m * base**i for i, m in enumerate(shifts))
 
     own_list = jnp.int32(listed(range(1, dm + 1)))
     for row in range(live_rows) if plan else ():
-        shifts = [m for m in order.get(row, range(1, dm + 1)) if home(row, m) == row]
+        shifts = [m for m in order.get(row, range(1, dm + 1)) if home(row, m) == row or (row, m) in halved]
         own_list = jnp.where(me == row, listed(shifts), own_list)
     own_list = jnp.where(live, own_list, 0)
 
@@ -372,9 +414,18 @@
 
         @pl.when(rest > 0)
         def _():
-            r_copy(m + 1, 0).wait_recv()
+            small = is_half(m, lambda row, _: row)
+
+            @pl.when(small)
+            def _():
+                half_copy(m + 1, 0).wait_recv()
+
+            @pl.when(jnp.logical_not(small))
+            def _():
+                r_copy(m + 1, 0).wait_recv()
+                column_sum(m, r_in[m], acc)
+
             right = r_in[m]
-            column_sum(m, right, acc)
             acc[HEAD:, :] += dot3(split(q_own[m]), split(right))
 
         return rest // base
@@ -386,11 +437,11 @@
         for c in range(CHUNKS):
             at = rows_of(c)
             if c < CHUNKS - 1:
-                for count in sorted({len(shifts) for _, shifts in plan.values()}):
-
-                    @pl.when(any_of(me, [device for device, shifts in plan.values() if len(shifts) == count]))
+                for count in sorted({units(row) for row in plan}):
+
+                    @pl.when(any_of(me, [plan[row][0] for row in plan if units(row) == count]))
                     def _():
-                        whole = (pl.ds(0, count), at)
+                        whole = q_units(count, at)
                         remote(qm.at[whole], q_far.at[whole], q_send.at[0], q_recv.at[c], 0).wait_recv()
 
             def far_step(step, rest):
@@ -404,9 +455,21 @@
                         rf_h[m], rf_l[m] = split(right)
                         column_sum(m, right, acc_far)
                     if c == CHUNKS - 1:
-                        here = (m, at)
                         slot = q_recv.at[CHUNKS - 1 + m]
-                        remote(qm.at[here], q_far.at[here], q_send.at[0], slot, 0).wait_recv()
+
+                        def wait_for(lanes):
+                            here = (m, at, pl.ds(0, lanes))
+                            remote(qm.at[here], q_far.at[here], q_send.at[0], slot, 0).wait_recv()
+
+                        small = is_half(m, lambda row, _: plan[row][0])
+
+                        @pl.when(small)
+                        def _():
+                            wait_for(half)
+
+                        @pl.when(jnp.logical_not(small))
+                        def _():
+                            wait_for(block)
                     acc_far[rows_of(c, HEAD), :] += dot3(split(q_far[m, at, :]), (rf_h[m], rf_l[m]))
 
                 return rest // base
@@ -444,8 +507,14 @@
 
         @pl.when(me == row)
         def _():
-            whole = pl.ds(0, len(shifts))
+            whole = q_units(units(row), pl.ds(0, block))
             remote(qm.at[whole], q_far.at[whole], q_send.at[0], q_recv.at[0], 0).wait_send()
+
+    for row, m in halved:
+
+        @pl.when(me == row + m)
+        def _():
+            half_copy(m, row).wait_send()
 
     @pl.when(me >= dist)
     def _():
@@ -465,33 +534,24 @@
             remote(relay_in.at[whole], relay_in.at[whole], relay_send.at[0], r_recv.at[0], 0).wait_send()
 
 
-def finish(live_rows, dist, acc, weight, row_sum, pair_out, branch_out, multi_out):
+def finish(dist, acc, weight, row_sum, pair_out, branch_out, multi_out):
     block = weight.shape[0]
     beta = 1.0 / (dist * block)
-    live = lax.axis_index("row") < live_rows
-
-    @pl.when(live)
-    def _():
-        column = lax.broadcasted_iota(jnp.int32, (block, 1), 0).astype(F32)
-        line = lax.broadcasted_iota(jnp.int32, (1, block), 1).astype(F32)
-        rows_i = lax.broadcasted_iota(jnp.int32, (block, block), 0)
-        cols_i = lax.broadcasted_iota(jnp.int32, (block, block), 1)
-        upper = jnp.where(cols_i >= rows_i, 1.0, 0.0).astype(BF16)
-        summed = acc[HEAD:, :]
-        pair = weight[...] * (1.0 + 0.8 * summed)
-        pair_out[...] = pair
-        high, low = split(pair * jnp.exp(line * beta))
-        inner = mm(high, upper) + mm(low, upper)
-        branch = (row_sum[:, 0:1] + inner) * (beta * jnp.exp(line * (-beta)))
-        branch_out[...] = branch
-        high, low = split(branch * jnp.exp(column * (-beta)))
-        tails = acc[0:1, :] + mm(upper, high) + mm(upper, low)
-        multi_out[...] = summed + 0.01 * jnp.exp(column * beta) * tails
-
-    @pl.when(jnp.logical_not(live))
-    def _():
-        for out in (pair_out, branch_out, multi_out):
-            out[...] = jnp.zeros_like(out)
+    column = lax.broadcasted_iota(jnp.int32, (block, 1), 0).astype(F32)
+    line = lax.broadcasted_iota(jnp.int32, (1, block), 1).astype(F32)
+    rows_i = lax.broadcasted_iota(jnp.int32, (block, block), 0)
+    cols_i = lax.broadcasted_iota(jnp.int32, (block, block), 1)
+    upper = jnp.where(cols_i >= rows_i, 1.0, 0.0).astype(BF16)
+    summed = acc[HEAD:, :]
+    pair = weight[...] * (1.0 + 0.8 * summed)
+    pair_out[...] = pair
+    high, low = split(pair * jnp.exp(line * beta))
+    inner = mm(high, upper) + mm(low, upper)
+    branch = (row_sum[:, 0:1] + inner) * (beta * jnp.exp(line * (-beta)))
+    branch_out[...] = branch
+    high, low = split(branch * jnp.exp(column * (-beta)))
+    tails = acc[0:1, :] + mm(upper, high) + mm(upper, low)
+    multi_out[...] = summed + 0.01 * jnp.exp(column * beta) * tails
 
 
 def solution(mesh):
@@ -529,7 +589,7 @@
                 pltpu.VMEM((1, turner.shape[0]), F32),
                 dma((1,)), dma((1,)), dma((CHUNKS - 1 + dm,)), dma((1,)), dma((dm,)), dma((dm,)),
                 dma((4,)), dma((2,)), dma((2,)),
-                pltpu.SemaphoreType.REGULAR((len(HELD),)),
+                pltpu.SemaphoreType.REGULAR((len(HELD),)), dma((1,)),
             ],
             compiler_params=pltpu.CompilerParams(has_side_effects=True, collective_id=0),
         )(
@@ -537,7 +597,7 @@
             codes[0], turner[None, :],
         )
         outs = pl.pallas_call(
-            functools.partial(finish, width - dist, dist),
+            functools.partial(finish, dist),
             out_shape=[square] * 3,
             in_specs=[local] * 3,
             out_specs=[local] * 3,

time: 30.4 us -> 30 us (0.987)
  no operation moved by 1% of the time
where the time goes in v6:
time: 30 us; the launch traced here: 29.8 us
  Pallas kernels  29.2 us (97%)
  between operations  0.64 us (2%)
    pallas_call x1, Pallas kernels, per_device(): pl.pallas_call(functools.partial(kernel, plan, relay, width), out_shape=[...  27.9 us
    pallas_call x1, Pallas kernels, per_device(): pl.pallas_call(functools.partial(finish, dist), out_shape=[square] * 3, i...  1.25 us

profile of v6, /device:TPU:8, one launch (start us, length us, event | category | flops | bytes accessed | tf_op | source)
XLA Modules:
  0.0 29.8 jit_solution(9106389559997563958)
XLA Ops:
  0.6 27.9 %shard_map.85 = (f32[264,256]{1,0:T(8,128)S(1)}, f32[256,256]{1,0:T(8,128)S(1)}, f32[256,128]{1,0:T(8,128)S(1)}) custom-call(f32[7,256,256]{2,1,0:T(8,128)} %bitcast.9, f32[7,256,256]{2,1,0:T(8,128)} %bitcast.10, f32[7,256,256]{2,1,0:T(8,128)} %bitcast.11, s32[256,256]{1,0:T(8,128)} %bitcast.12, s32[1,256]{1,0:T(1,128)} %bitcast.13, f32[1,64]{1,0:T(1,128)} %bitcast.14), custom_call_target="tpu_custom_call" | custom-call | tf_op jit(solution)/shard_map/pallas_call | solution.py:574
  28.5 1.3 %shard_map.86 = (f32[256,256]{1,0:T(8,128)}, f32[256,256]{1,0:T(8,128)}, f32[256,256]{1,0:T(8,128)}) custom-call(f32[264,256]{1,0:T(8,128)S(1)} %get-tuple-element.9.acc, f32[256,256]{1,0:T(8,128)S(1)} %get-tuple-element.10.weight, f32[256,128]{1,0:T(8,128)S(1)} %get-tuple-element.11.row_sum), custom_call_target="tpu_custom_call" | custom-call | tf_op jit(solution)/shard_map/pallas_call | solution.py:599

commit v7 on v6

--- a/solution.py
+++ b/solution.py
@@ -18,21 +18,22 @@
     7: (11, (4, 3, 7, 1, 2, 5, 6)),
 }
 RELAY = {
-    (6, 7): (15, 4, 0),
-    (6, 6): (14, 4, 0),
+    (6, 7): (15, 4, 1),
+    (6, 6): (14, 4, 1),
     (2, 6): (10, 4, 0),
     (6, 2): (10, 1, 4),
     (6, 3): (10, 4, 0),
-    (7, 5): (14, 4, 1),
-    (7, 6): (15, 4, 1),
+    (7, 5): (14, 4, 0),
+    (7, 6): (15, 4, 0),
 }
 HELD = (
     {4: (6,), 5: (6,), 8: (10, 11), 9: (10, 11)},
     {4: (2,), 5: (2,), 8: (2, 6), 9: (2, 6)},
 )
-SPLIT = ((5, 3),)
+SPLIT = ((4, 4),)
 ORDER = {6: (1, 7, 6, 5, 4, 3, 2)}
-SHARES = (4, 2, 1, 1)
+DETOUR = {(5, 7): 6}
+SHARES = (8, 4, 3, 1)
 CHUNKS = len(SHARES)
 PIECES = 4
 HEAD = 8
@@ -61,9 +62,9 @@
 
 
 def kernel(
-    plan, relay, width, qm, qm1, qb, eidx, codes, turner, acc, weight, row_sum,
-    q_own, r_in, r_far, q_far, rf_h, rf_l, qb_in, e_in, code_in, acc_far, partial_in, relay_in, code_own, table_in,
-    own_sem, q_send, q_recv, r_send, r_recv, rf_recv, load_sem, code_sem, part_sem, held_sem, half_sem,
+    plan, relay, width, qm, qm1, qb, eidx, codes, turner, acc, weight, row_sum, partial_in,
+    q_own, r_in, r_far, q_far, rf_h, rf_l, qb_in, e_in, code_in, acc_far, relay_in, code_own, table_in,
+    own_sem, q_send, q_recv, r_send, r_recv, rf_recv, load_sem, code_sem, part_sem, held_sem,
 ):
     dm, block = qm.shape[0], qm.shape[1]
     dist = dm + 1
@@ -75,6 +76,7 @@
     relay_send, relay_recv = q_send, q_recv
     unit = block // sum(SHARES)
     piece = block // PIECES
+    side = block // 8
 
     def remote(src, dst, send, recv, device):
         return pltpu.make_async_remote_copy(
@@ -92,6 +94,7 @@
     held = HELD if plan else ()
     order = ORDER if plan else {}
     halved = SPLIT if plan else ()
+    detour = DETOUR if plan else {}
     half = block // 2
     waiting = []
     for group in held:
@@ -108,6 +111,10 @@
         waiting.append(lists)
     for row, m in halved:
         waiting[-1][row + m].insert(1, (row, m, "half"))
+    for (row, m), via in detour.items():
+        for n, group in enumerate(held):
+            if via in group.get(row, ()):
+                waiting[n][row].insert(0, (row, m, "detour"))
     kinds = [item for lists in waiting for keys in lists.values() for item in keys]
     rests = {(row, m) for row, m, kind in kinds if kind == "rest"}
     parts = {(row, m) for row, m, kind in kinds if kind == "relay"}
@@ -139,7 +146,10 @@
         return pl.ds(sum(SHARES[:c]) * unit + shift, SHARES[c] * unit)
 
     def q_copy(row, m, c, device):
-        at = (m - 1, rows_of(c), pl.ds(0, half if (row, m) in halved else block))
+        rows = rows_of(c)
+        if c == 0 and (row, m) in detour:
+            rows = pl.ds(side, SHARES[0] * unit - side)
+        at = (m - 1, rows, pl.ds(0, half if (row, m) in halved else block))
         slot = c if c < CHUNKS - 1 else CHUNKS - 2 + m
         return remote(qm.at[at], q_far.at[at], q_send.at[0], q_recv.at[slot], device)
 
@@ -149,9 +159,15 @@
     def rf_copy(m, device):
         return remote(qm1.at[dm - m], r_far.at[m - 1], r_send.at[0], rf_recv.at[m - 1], device)
 
+    def detour_copy(m, via):
+        return remote(qm.at[m - 1, pl.ds(0, side)], relay_in.at[0, pl.ds(0, side)], q_send.at[0], code_sem.at[0], via)
+
+    def detour_on(m, device):
+        return remote(relay_in.at[0, pl.ds(0, side)], q_far.at[m - 1, pl.ds(0, side)], q_send.at[0], q_recv.at[0], device)
+
     def half_copy(m, device):
         at = pl.ds(half, block - half)
-        return remote(qm1.at[dm - m, at], r_in.at[m - 1, at], half_sem.at[0], r_recv.at[m - 1], device)
+        return remote(qm1.at[dm - m, at], r_in.at[m - 1, at], q_send.at[0], r_recv.at[m - 1], device)
 
     def units(row):
         shifts = plan[row][1]
@@ -204,6 +220,8 @@
                             relay_copy(row, m, p).start()
                     elif kind == "half":
                         half_copy(m, row).start()
+                    elif kind == "detour":
+                        detour_copy(m, detour[row, m]).start()
                     else:
                         held_send(row, m)
 
@@ -233,6 +251,8 @@
                     pairs.add((source, row))
         for row, (device, _) in plan.items():
             pairs |= {(row, device), (device, row)}
+        for (row, m), via in detour.items():
+            pairs |= {(row, via), (via, plan[row][0])}
         for group in held:
             for source, devices in group.items():
                 pairs -= {(source, device) for device in devices}
@@ -330,6 +350,12 @@
 
     if held:
         send_held(0)
+    for (row, m), via in detour.items():
+
+        @pl.when(me == via)
+        def _():
+            detour_copy(m, 0).wait_recv()
+            detour_on(m, plan[row][0]).start()
 
     for via in sorted({via for via, _, _ in relay.values()}):
 
@@ -351,6 +377,10 @@
         @pl.when(me == row)
         def _():
             r_in[m - 1, 0:half, :] = jnp.zeros((half, block), F32)
+
+    @pl.when(jnp.logical_not(any_of(me, list(plan))) if plan else me >= 0)
+    def _():
+        partial_in[...] = jnp.zeros_like(partial_in)
 
     @pl.when(jnp.logical_not(live))
     def _():
@@ -488,7 +518,6 @@
         @pl.when(any_of(me, list(plan)))
         def _():
             remote(acc_far, partial_in, part_sem.at[0], part_sem.at[1], 0).wait_recv()
-            acc[...] += partial_in[...]
 
     sent = jnp.int32(0)
     for m in range(1, dist):
@@ -516,6 +545,12 @@
         def _():
             half_copy(m, row).wait_send()
 
+    for (_, m), via in detour.items():
+
+        @pl.when(me == via)
+        def _():
+            detour_on(m, 0).wait_send()
+
     @pl.when(me >= dist)
     def _():
         code_send().wait_send()
@@ -534,7 +569,7 @@
             remote(relay_in.at[whole], relay_in.at[whole], relay_send.at[0], r_recv.at[0], 0).wait_send()
 
 
-def finish(dist, acc, weight, row_sum, pair_out, branch_out, multi_out):
+def finish(dist, acc, weight, row_sum, partial, pair_out, branch_out, multi_out):
     block = weight.shape[0]
     beta = 1.0 / (dist * block)
     column = lax.broadcasted_iota(jnp.int32, (block, 1), 0).astype(F32)
@@ -542,7 +577,7 @@
     rows_i = lax.broadcasted_iota(jnp.int32, (block, block), 0)
     cols_i = lax.broadcasted_iota(jnp.int32, (block, block), 1)
     upper = jnp.where(cols_i >= rows_i, 1.0, 0.0).astype(BF16)
-    summed = acc[HEAD:, :]
+    summed = acc[HEAD:, :] + partial[HEAD:, :]
     pair = weight[...] * (1.0 + 0.8 * summed)
     pair_out[...] = pair
     high, low = split(pair * jnp.exp(line * beta))
@@ -550,7 +585,7 @@
     branch = (row_sum[:, 0:1] + inner) * (beta * jnp.exp(line * (-beta)))
     branch_out[...] = branch
     high, low = split(branch * jnp.exp(column * (-beta)))
-    tails = acc[0:1, :] + mm(upper, high) + mm(upper, low)
+    tails = acc[0:1, :] + partial[0:1, :] + mm(upper, high) + mm(upper, low)
     multi_out[...] = summed + 0.01 * jnp.exp(column * beta) * tails
 
 
@@ -577,19 +612,20 @@
                 pltpu.VMEM((block + HEAD, block), F32),
                 pltpu.VMEM((block, block), F32),
                 pltpu.VMEM((block, 128), F32),
+                tall,
             ],
             in_specs=[anywhere] * 6,
-            out_specs=[local] * 3,
+            out_specs=[local] * 4,
             scratch_shapes=[
                 blocks, blocks, blocks, blocks, halves, halves, blocks,
                 pltpu.VMEM((block, block), jnp.int32),
                 pltpu.VMEM((1, block), jnp.int32),
-                tall, tall, pltpu.VMEM((pieces, block // PIECES, block), F32),
+                tall, pltpu.VMEM((pieces, block // PIECES, block), F32),
                 pltpu.VMEM((1, block), jnp.int32),
                 pltpu.VMEM((1, turner.shape[0]), F32),
                 dma((1,)), dma((1,)), dma((CHUNKS - 1 + dm,)), dma((1,)), dma((dm,)), dma((dm,)),
                 dma((4,)), dma((2,)), dma((2,)),
-                pltpu.SemaphoreType.REGULAR((len(HELD),)), dma((1,)),
+                pltpu.SemaphoreType.REGULAR((len(HELD),)),
             ],
             compiler_params=pltpu.CompilerParams(has_side_effects=True, collective_id=0),
         )(
@@ -599,7 +635,7 @@
         outs = pl.pallas_call(
             functools.partial(finish, dist),
             out_shape=[square] * 3,
-            in_specs=[local] * 3,
+            in_specs=[local] * 4,
             out_specs=[local] * 3,
             compiler_params=pltpu.CompilerParams(vmem_limit_bytes=16 * 2**20),
         )(*middle)

time: 30 us -> 30 us (level); the launches traced: 29.8 us -> 29.4 us
  Pallas kernels: 29.2 us -> 28.8 us
    pallas_call x1, Pallas kernels: 27.9 us -> 27.5 us  [per_device(): pl.pallas_call(functools.partial(kernel, plan, relay, width), out_shape=[...]
where the time goes in v7:
time: 30 us; the launch traced here: 29.4 us
  Pallas kernels  28.8 us (96%)
  between operations  0.64 us (2%)
    pallas_call x1, Pallas kernels, per_device(): pl.pallas_call(functools.partial(kernel, plan, relay, width), out_shape=[...  27.5 us
    pallas_call x1, Pallas kernels, per_device(): pl.pallas_call(functools.partial(finish, dist), out_shape=[square] * 3, i...  1.26 us

profile of v7, /device:TPU:8, one launch (start us, length us, event | category | flops | bytes accessed | tf_op | source)
XLA Modules:
  0.0 29.4 jit_solution(1936584594224469617)
XLA Ops:
  0.6 27.5 %shard_map.85 = (f32[264,256]{1,0:T(8,128)S(1)}, f32[256,256]{1,0:T(8,128)S(1)}, f32[256,128]{1,0:T(8,128)S(1)}, f32[264,256]{1,0:T(8,128)S(1)}) custom-call(f32[7,256,256]{2,1,0:T(8,128)} %bitcast.9, f32[7,256,256]{2,1,0:T(8,128)} %bitcast.10, f32[7,256,256]{2,1,0:T(8,128)} %bitcast.11, s32[256,256]{1,0:T(8,128)} %bitcast.12, s32[1,256]{1,0:T(1,128)} %bitcast.13, ...), custom_call_target="tpu_custom_call" | custom-call | tf_op jit(solution)/shard_map/pallas_call | solution.py:609
  28.2 1.3 %shard_map.86 = (f32[256,256]{1,0:T(8,128)}, f32[256,256]{1,0:T(8,128)}, f32[256,256]{1,0:T(8,128)}) custom-call(f32[264,256]{1,0:T(8,128)S(1)} %get-tuple-element.10.acc, f32[256,256]{1,0:T(8,128)S(1)} %get-tuple-element.11.weight, f32[256,128]{1,0:T(8,128)S(1)} %get-tuple-element.12.row_sum, f32[264,256]{1,0:T(8,128)S(1)} %get-tuple-element.13.partial), custom_call_target="tpu_custom_call" | custom-call | tf_op jit(solution)/shard_map/pallas_call | solution.py:635

commit v8 on v7

--- a/solution.py
+++ b/solution.py
@@ -18,13 +18,13 @@
     7: (11, (4, 3, 7, 1, 2, 5, 6)),
 }
 RELAY = {
-    (6, 7): (15, 4, 1),
-    (6, 6): (14, 4, 1),
+    (6, 7): (15, 4, 0),
+    (6, 6): (14, 4, 0),
     (2, 6): (10, 4, 0),
     (6, 2): (10, 1, 4),
     (6, 3): (10, 4, 0),
-    (7, 5): (14, 4, 0),
-    (7, 6): (15, 4, 0),
+    (7, 5): (14, 4, 2),
+    (7, 6): (15, 4, 2),
 }
 HELD = (
     {4: (6,), 5: (6,), 8: (10, 11), 9: (10, 11)},
@@ -107,7 +107,7 @@
                     lists[source].append((row, m, "rest"))
                 if via in group[source]:
                     lists[source].append((row, m, "relay"))
-            lists[source].sort(key=lambda item: (item[2] == "relay", item[0] not in (3, 7), -item[0]))
+            lists[source].sort(key=lambda item: (item[2] != "relay", item[0] not in (3, 7), -item[0]))
         waiting.append(lists)
     for row, m in halved:
         waiting[-1][row + m].insert(1, (row, m, "half"))

time: 30 us -> 29.6 us (0.987); the launches traced: 29.4 us -> 29.4 us
  no operation moved by 1% of the time
where the time goes in v8:
time: 29.6 us; the launch traced here: 29.4 us
  Pallas kernels  28.8 us (97%)
  between operations  0.64 us (2%)
    pallas_call x1, Pallas kernels, per_device(): pl.pallas_call(functools.partial(kernel, plan, relay, width), out_shape=[...  27.5 us
    pallas_call x1, Pallas kernels, per_device(): pl.pallas_call(functools.partial(finish, dist), out_shape=[square] * 3, i...  1.26 us

profile of v8, /device:TPU:8, one launch (start us, length us, event | category | flops | bytes accessed | tf_op | source)
XLA Modules:
  0.0 29.4 jit_solution(17746142352910952137)
XLA Ops:
  0.6 27.5 %shard_map.85 = (f32[264,256]{1,0:T(8,128)S(1)}, f32[256,256]{1,0:T(8,128)S(1)}, f32[256,128]{1,0:T(8,128)S(1)}, f32[264,256]{1,0:T(8,128)S(1)}) custom-call(f32[7,256,256]{2,1,0:T(8,128)} %bitcast.9, f32[7,256,256]{2,1,0:T(8,128)} %bitcast.10, f32[7,256,256]{2,1,0:T(8,128)} %bitcast.11, s32[256,256]{1,0:T(8,128)} %bitcast.12, s32[1,256]{1,0:T(1,128)} %bitcast.13, ...), custom_call_target="tpu_custom_call" | custom-call | tf_op jit(solution)/shard_map/pallas_call | solution.py:609
  28.2 1.3 %shard_map.86 = (f32[256,256]{1,0:T(8,128)}, f32[256,256]{1,0:T(8,128)}, f32[256,256]{1,0:T(8,128)}) custom-call(f32[264,256]{1,0:T(8,128)S(1)} %get-tuple-element.10.acc, f32[256,256]{1,0:T(8,128)S(1)} %get-tuple-element.11.weight, f32[256,128]{1,0:T(8,128)S(1)} %get-tuple-element.12.row_sum, f32[264,256]{1,0:T(8,128)S(1)} %get-tuple-element.13.partial), custom_call_target="tpu_custom_call" | custom-call | tf_op jit(solution)/shard_map/pallas_call | solution.py:635

commit v9 on v8

--- a/solution.py
+++ b/solution.py
@@ -30,11 +30,13 @@
     {4: (6,), 5: (6,), 8: (10, 11), 9: (10, 11)},
     {4: (2,), 5: (2,), 8: (2, 6), 9: (2, 6)},
 )
-SPLIT = ((4, 4),)
+SPLIT = ()
 ORDER = {6: (1, 7, 6, 5, 4, 3, 2)}
-DETOUR = {(5, 7): 6}
+DETOUR = {(4, 7): (6, 7), (5, 7): (6, 2)}
+AFTER = {8: ((6, 2),)}
 SHARES = (8, 4, 3, 1)
 CHUNKS = len(SHARES)
+COARSE = 2
 PIECES = 4
 HEAD = 8
 
@@ -63,7 +65,7 @@
 
 def kernel(
     plan, relay, width, qm, qm1, qb, eidx, codes, turner, acc, weight, row_sum, partial_in,
-    q_own, r_in, r_far, q_far, rf_h, rf_l, qb_in, e_in, code_in, acc_far, relay_in, code_own, table_in,
+    q_own, r_in, r_far, q_far, rf_h, rf_l, qb_in, e_in, code_in, acc_far, relay_in, detour_in, code_own, table_in,
     own_sem, q_send, q_recv, r_send, r_recv, rf_recv, load_sem, code_sem, part_sem, held_sem,
 ):
     dm, block = qm.shape[0], qm.shape[1]
@@ -76,7 +78,6 @@
     relay_send, relay_recv = q_send, q_recv
     unit = block // sum(SHARES)
     piece = block // PIECES
-    side = block // 8
 
     def remote(src, dst, send, recv, device):
         return pltpu.make_async_remote_copy(
@@ -95,6 +96,12 @@
     order = ORDER if plan else {}
     halved = SPLIT if plan else ()
     detour = DETOUR if plan else {}
+    after = AFTER if plan else {}
+    sides, edge = {}, 0
+    for key, (_, share) in detour.items():
+        sides[key] = (edge, share * block // 16)
+        edge += share * block // 16
+    last = {key for keys in after.values() for key in keys}
     half = block // 2
     waiting = []
     for group in held:
@@ -103,7 +110,7 @@
             for row in range(min(live_rows, source) - 1, max(source - dist, -1), -1):
                 m = source - row
                 via, count, _ = relay.get((row, m), (None, 0, 0))
-                if home(row, m) in group[source] and count < PIECES:
+                if home(row, m) in group[source] and count < PIECES and (row, m) not in last:
                     lists[source].append((row, m, "rest"))
                 if via in group[source]:
                     lists[source].append((row, m, "relay"))
@@ -111,12 +118,12 @@
         waiting.append(lists)
     for row, m in halved:
         waiting[-1][row + m].insert(1, (row, m, "half"))
-    for (row, m), via in detour.items():
+    for (row, m), (via, _) in detour.items():
         for n, group in enumerate(held):
             if via in group.get(row, ()):
                 waiting[n][row].insert(0, (row, m, "detour"))
     kinds = [item for lists in waiting for keys in lists.values() for item in keys]
-    rests = {(row, m) for row, m, kind in kinds if kind == "rest"}
+    rests = last | {(row, m) for row, m, kind in kinds if kind == "rest"}
     parts = {(row, m) for row, m, kind in kinds if kind == "relay"}
 
     def apart(m):
@@ -148,9 +155,10 @@
     def q_copy(row, m, c, device):
         rows = rows_of(c)
         if c == 0 and (row, m) in detour:
-            rows = pl.ds(side, SHARES[0] * unit - side)
+            start = sides[row, m][1]
+            rows = pl.ds(start, SHARES[0] * unit - start)
         at = (m - 1, rows, pl.ds(0, half if (row, m) in halved else block))
-        slot = c if c < CHUNKS - 1 else CHUNKS - 2 + m
+        slot = c if c < COARSE else COARSE + (c - COARSE) * dm + m - 1
         return remote(qm.at[at], q_far.at[at], q_send.at[0], q_recv.at[slot], device)
 
     def r_copy(m, device):
@@ -159,11 +167,22 @@
     def rf_copy(m, device):
         return remote(qm1.at[dm - m], r_far.at[m - 1], r_send.at[0], rf_recv.at[m - 1], device)
 
-    def detour_copy(m, via):
-        return remote(qm.at[m - 1, pl.ds(0, side)], relay_in.at[0, pl.ds(0, side)], q_send.at[0], code_sem.at[0], via)
-
-    def detour_on(m, device):
-        return remote(relay_in.at[0, pl.ds(0, side)], q_far.at[m - 1, pl.ds(0, side)], q_send.at[0], q_recv.at[0], device)
+    def detour_copy(row, m):
+        start, size = sides[row, m]
+        return remote(
+            qm.at[m - 1, pl.ds(0, size)], detour_in.at[pl.ds(start, size)],
+            q_send.at[0], code_sem.at[0], detour[row, m][0],
+        )
+
+    def detour_on(row, m):
+        start, size = sides[row, m]
+        return remote(
+            detour_in.at[pl.ds(start, size)], q_far.at[m - 1, pl.ds(0, size)],
+            q_send.at[0], q_recv.at[0], plan[row][0],
+        )
+
+    def detour_all():
+        return remote(detour_in.at[pl.ds(0, edge)], detour_in.at[pl.ds(0, edge)], q_send.at[0], code_sem.at[0], 0)
 
     def half_copy(m, device):
         at = pl.ds(half, block - half)
@@ -221,7 +240,7 @@
                     elif kind == "half":
                         half_copy(m, row).start()
                     elif kind == "detour":
-                        detour_copy(m, detour[row, m]).start()
+                        detour_copy(row, m).start()
                     else:
                         held_send(row, m)
 
@@ -251,7 +270,7 @@
                     pairs.add((source, row))
         for row, (device, _) in plan.items():
             pairs |= {(row, device), (device, row)}
-        for (row, m), via in detour.items():
+        for (row, m), (via, _) in detour.items():
             pairs |= {(row, via), (via, plan[row][0])}
         for group in held:
             for source, devices in group.items():
@@ -350,12 +369,13 @@
 
     if held:
         send_held(0)
-    for (row, m), via in detour.items():
+    for via in sorted({via for via, _ in detour.values()}):
 
         @pl.when(me == via)
         def _():
-            detour_copy(m, 0).wait_recv()
-            detour_on(m, plan[row][0]).start()
+            detour_all().wait_recv()
+            for row, m in detour:
+                detour_on(row, m).start()
 
     for via in sorted({via for via, _, _ in relay.values()}):
 
@@ -466,7 +486,7 @@
             far_list = far_list + jnp.where(me == device, listed(shifts), 0)
         for c in range(CHUNKS):
             at = rows_of(c)
-            if c < CHUNKS - 1:
+            if c < COARSE:
                 for count in sorted({units(row) for row in plan}):
 
                     @pl.when(any_of(me, [plan[row][0] for row in plan if units(row) == count]))
@@ -484,8 +504,8 @@
                         right = r_far[m]
                         rf_h[m], rf_l[m] = split(right)
                         column_sum(m, right, acc_far)
-                    if c == CHUNKS - 1:
-                        slot = q_recv.at[CHUNKS - 1 + m]
+                    if c >= COARSE:
+                        slot = q_recv.at[COARSE + (c - COARSE) * dm + m]
 
                         def wait_for(lanes):
                             here = (m, at, pl.ds(0, lanes))
@@ -510,6 +530,13 @@
                 @pl.when(me == device)
                 def _():
                     part_copy(c, row).start()
+
+            for source, keys in after.items() if c == 0 else ():
+
+                @pl.when(me == source)
+                def _():
+                    for row, m in keys:
+                        held_send(row, m)
 
     lax.fori_loop(0, dm, own_step, own_list)
 
@@ -545,11 +572,11 @@
         def _():
             half_copy(m, row).wait_send()
 
-    for (_, m), via in detour.items():
+    for via in sorted({via for via, _ in detour.values()}):
 
         @pl.when(me == via)
         def _():
-            detour_on(m, 0).wait_send()
+            detour_all().wait_send()
 
     @pl.when(me >= dist)
     def _():
@@ -621,9 +648,10 @@
                 pltpu.VMEM((block, block), jnp.int32),
                 pltpu.VMEM((1, block), jnp.int32),
                 tall, pltpu.VMEM((pieces, block // PIECES, block), F32),
+                pltpu.VMEM((block, block), F32),
                 pltpu.VMEM((1, block), jnp.int32),
                 pltpu.VMEM((1, turner.shape[0]), F32),
-                dma((1,)), dma((1,)), dma((CHUNKS - 1 + dm,)), dma((1,)), dma((dm,)), dma((dm,)),
+                dma((1,)), dma((1,)), dma((COARSE + (CHUNKS - COARSE) * dm,)), dma((1,)), dma((dm,)), dma((dm,)),
                 dma((4,)), dma((2,)), dma((2,)),
                 pltpu.SemaphoreType.REGULAR((len(HELD),)),
             ],

time: 29.6 us -> 29.6 us (level)
  no operation moved by 1% of the time
where the time goes in v9:
time: 29.6 us; the launch traced here: 29.4 us
  Pallas kernels  28.8 us (97%)
  between operations  0.64 us (2%)
    pallas_call x1, Pallas kernels, per_device(): pl.pallas_call(functools.partial(kernel, plan, relay, width), out_shape=[...  27.5 us
    pallas_call x1, Pallas kernels, per_device(): pl.pallas_call(functools.partial(finish, dist), out_shape=[square] * 3, i...  1.26 us

profile of v9, /device:TPU:8, one launch (start us, length us, event | category | flops | bytes accessed | tf_op | source)
XLA Modules:
  0.0 29.4 jit_solution(3673654414496724834)
XLA Ops:
  0.6 27.5 %shard_map.85 = (f32[264,256]{1,0:T(8,128)S(1)}, f32[256,256]{1,0:T(8,128)S(1)}, f32[256,128]{1,0:T(8,128)S(1)}, f32[264,256]{1,0:T(8,128)S(1)}) custom-call(f32[7,256,256]{2,1,0:T(8,128)} %bitcast.9, f32[7,256,256]{2,1,0:T(8,128)} %bitcast.10, f32[7,256,256]{2,1,0:T(8,128)} %bitcast.11, s32[256,256]{1,0:T(8,128)} %bitcast.12, s32[1,256]{1,0:T(1,128)} %bitcast.13, ...), custom_call_target="tpu_custom_call" | custom-call | tf_op jit(solution)/shard_map/pallas_call | solution.py:636
  28.1 1.3 %shard_map.86 = (f32[256,256]{1,0:T(8,128)}, f32[256,256]{1,0:T(8,128)}, f32[256,256]{1,0:T(8,128)}) custom-call(f32[264,256]{1,0:T(8,128)S(1)} %get-tuple-element.10.acc, f32[256,256]{1,0:T(8,128)S(1)} %get-tuple-element.11.weight, f32[256,128]{1,0:T(8,128)S(1)} %get-tuple-element.12.row_sum, f32[264,256]{1,0:T(8,128)S(1)} %get-tuple-element.13.partial), custom_call_target="tpu_custom_call" | custom-call | tf_op jit(solution)/shard_map/pallas_call | solution.py:663

commit v10 on v9

--- a/solution.py
+++ b/solution.py
@@ -34,6 +34,7 @@
 ORDER = {6: (1, 7, 6, 5, 4, 3, 2)}
 DETOUR = {(4, 7): (6, 7), (5, 7): (6, 2)}
 AFTER = {8: ((6, 2),)}
+FIRST = (7, 6, 11, 10, 4, 5, 9, 8, 2)
 SHARES = (8, 4, 3, 1)
 CHUNKS = len(SHARES)
 COARSE = 2
@@ -126,25 +127,11 @@
     rests = last | {(row, m) for row, m, kind in kinds if kind == "rest"}
     parts = {(row, m) for row, m, kind in kinds if kind == "relay"}
 
-    def apart(m):
-        if not plan:
-            return []
-        return [
-            row for row in range(live_rows)
-            if (row, m) in relay or (row, m) in rests or home(row, m) != row
-        ]
-
     def held_send(row, m):
         if (row, m) in relay:
             relay_rest(row, m).start()
         else:
             (r_copy if home(row, m) == row else rf_copy)(m, home(row, m)).start()
-
-    def direct(m):
-        row = me - m
-        ok = near(row)
-        rows = apart(m)
-        return jnp.logical_and(ok, jnp.logical_not(any_of(row, rows))) if rows else ok
 
     def code_send():
         return remote(codes, code_in, code_sem.at[0], code_sem.at[1], me - dist)
@@ -278,9 +265,11 @@
                 pairs |= {(device, source) for device in devices}
         pairs = sorted((s, d) for s, d in pairs if s != d)
         awaited = jnp.int32(0)
+        ranked = [*FIRST, *(device for device in range(width) if device not in FIRST)]
         for device in range(width):
+            awaited = awaited + jnp.where(me == device, sum(1 for s, _ in pairs if s == device), 0)
+        for device in ranked:
             sources = [s for s, d in pairs if d == device]
-            awaited = awaited + jnp.where(me == device, sum(1 for s, _ in pairs if s == device), 0)
             if sources:
 
                 @pl.when(me == device)
@@ -303,56 +292,56 @@
     def _():
         pl.semaphore_wait(barrier, awaited)
 
-    for n, group in enumerate(held):
-        for device in sorted({device for devices in group.values() for device in devices}):
+    def starts(device):
+        found = []
+        device_of, shifts = plan.get(device, (None, ()))
+        found += [q_copy(device, m, 0, device_of) for m in shifts]
+        for m in range(dm, 0, -1):
+            row = device - m
+            if 0 <= row < live_rows and home(row, m) != row and (row, m) not in relay and (row, m) not in rests:
+                if home(row, m) == device:
+                    found.append(pltpu.make_async_copy(qm1.at[dm - m], r_far.at[m - 1], rf_recv.at[m - 1]))
+                else:
+                    found.append(rf_copy(m, home(row, m)))
+        for row, m, p in slots:
+            if row + m == device and (row, m) not in parts:
+                found.append(relay_copy(row, m, p))
+        for (row, m), (_, count, _) in relay.items():
+            if row + m == device and count < PIECES and (row, m) not in rests:
+                found.append(relay_rest(row, m))
+        for m in range(dm, 0, -1):
+            row = device - m
+            if 0 <= row < live_rows and home(row, m) == row and (row, m) not in relay and (row, m) not in rests:
+                found.append(r_copy(m, row))
+        found += [q_copy(device, m, c, device_of) for c in range(1, CHUNKS) for m in shifts]
+        return found
+
+    if plan:
+        for device in ranked:
 
             @pl.when(me == device)
             def _():
-                for source in [source for source, devices in group.items() if device in devices]:
-                    pl.semaphore_signal(
-                        held_sem.at[n], inc=1, device_id={"row": source}, device_id_type=pl.DeviceIdType.MESH
-                    )
-
-    @pl.when(me >= dist)
-    def _():
-        code_send().start()
-
-    for m in range(dm, 0, -1):
-        for row, (device, shifts) in plan.items():
-            if m not in shifts or (row, m) in relay or (row, m) in rests:
-                continue
-
-            @pl.when(me == row + m)
+                for n, group in enumerate(held):
+                    for source in [source for source, devices in group.items() if device in devices]:
+                        pl.semaphore_signal(
+                            held_sem.at[n], inc=1, device_id={"row": source}, device_id_type=pl.DeviceIdType.MESH
+                        )
+                if device >= dist:
+                    code_send().start()
+                for copy in starts(device):
+                    copy.start()
+
+    if not plan:
+
+        @pl.when(me >= dist)
+        def _():
+            code_send().start()
+
+        for m in range(dm, 0, -1):
+
+            @pl.when(near(me - m))
             def _():
-                if row + m == device:
-                    pltpu.make_async_copy(qm1.at[dm - m], r_far.at[m - 1], rf_recv.at[m - 1]).start()
-                else:
-                    rf_copy(m, device).start()
-
-    for row, (device, shifts) in plan.items():
-
-        @pl.when(me == row)
-        def _():
-            for c in range(CHUNKS):
-                for m in shifts:
-                    q_copy(row, m, c, device).start()
-
-    for source in sorted({row + m for row, m in relay}):
-
-        @pl.when(me == source)
-        def _():
-            for row, m, p in slots:
-                if row + m == source and (row, m) not in parts:
-                    relay_copy(row, m, p).start()
-            for (row, m), (_, count, _) in relay.items():
-                if row + m == source and count < PIECES and (row, m) not in rests:
-                    relay_rest(row, m).start()
-
-    for m in range(dm, 0, -1):
-
-        @pl.when(direct(m))
-        def _():
-            r_copy(m, me - m).start()
+                r_copy(m, me - m).start()
 
     loads = (
         pltpu.make_async_copy(qb, qb_in, load_sem.at[0]),

time: 29.6 us -> 29.5 us (level)
  no operation moved by 1% of the time
where the time goes in v10:
time: 29.5 us; the launch traced here: 29.4 us
  Pallas kernels  28.7 us (97%)
  between operations  0.64 us (2%)
    pallas_call x1, Pallas kernels, per_device(): pl.pallas_call(functools.partial(kernel, plan, relay, width), out_shape=[...  27.5 us
    pallas_call x1, Pallas kernels, per_device(): pl.pallas_call(functools.partial(finish, dist), out_shape=[square] * 3, i...  1.26 us

profile of v10, /device:TPU:8, one launch (start us, length us, event | category | flops | bytes accessed | tf_op | source)
XLA Modules:
  0.0 29.4 jit_solution(10733004693097761943)
XLA Ops:
  0.6 27.5 %shard_map.85 = (f32[264,256]{1,0:T(8,128)S(1)}, f32[256,256]{1,0:T(8,128)S(1)}, f32[256,128]{1,0:T(8,128)S(1)}, f32[264,256]{1,0:T(8,128)S(1)}) custom-call(f32[7,256,256]{2,1,0:T(8,128)} %bitcast.9, f32[7,256,256]{2,1,0:T(8,128)} %bitcast.10, f32[7,256,256]{2,1,0:T(8,128)} %bitcast.11, s32[256,256]{1,0:T(8,128)} %bitcast.12, s32[1,256]{1,0:T(1,128)} %bitcast.13, ...), custom_call_target="tpu_custom_call" | custom-call | tf_op jit(solution)/shard_map/pallas_call | solution.py:625
  28.1 1.3 %shard_map.86 = (f32[256,256]{1,0:T(8,128)}, f32[256,256]{1,0:T(8,128)}, f32[256,256]{1,0:T(8,128)}) custom-call(f32[264,256]{1,0:T(8,128)S(1)} %get-tuple-element.10.acc, f32[256,256]{1,0:T(8,128)S(1)} %get-tuple-element.11.weight, f32[256,128]{1,0:T(8,128)S(1)} %get-tuple-element.12.row_sum, f32[264,256]{1,0:T(8,128)S(1)} %get-tuple-element.13.partial), custom_call_target="tpu_custom_call" | custom-call | tf_op jit(solution)/shard_map/pallas_call | solution.py:652

commit v11 on v10

--- a/solution.py
+++ b/solution.py
@@ -12,7 +12,7 @@
 
 PLAN = {
     1: (5, (4, 3, 6, 5, 7)),
-    3: (6, (3, 1, 2, 7, 6, 5)),
+    3: (6, (3, 2, 7, 6, 5)),
     4: (8, (4, 5, 7, 6)),
     5: (9, (3, 6, 5, 7)),
     7: (11, (4, 3, 7, 1, 2, 5, 6)),
@@ -21,7 +21,6 @@
     (6, 7): (15, 4, 0),
     (6, 6): (14, 4, 0),
     (2, 6): (10, 4, 0),
-    (6, 2): (10, 1, 4),
     (6, 3): (10, 4, 0),
     (7, 5): (14, 4, 2),
     (7, 6): (15, 4, 2),
@@ -32,8 +31,8 @@
 )
 SPLIT = ()
 ORDER = {6: (1, 7, 6, 5, 4, 3, 2)}
-DETOUR = {(4, 7): (6, 7), (5, 7): (6, 2)}
-AFTER = {8: ((6, 2),)}
+DETOUR = {(4, 7): (6, 7), (4, 6): (6, 2)}
+AFTER = {}
 FIRST = (7, 6, 11, 10, 4, 5, 9, 8, 2)
 SHARES = (8, 4, 3, 1)
 CHUNKS = len(SHARES)

time: 29.5 us -> 29.1 us (0.986)
  Pallas kernels: 28.7 us -> 28.3 us
    pallas_call x1, Pallas kernels: 27.5 us -> 27 us  [per_device(): pl.pallas_call(functools.partial(kernel, plan, relay, width), out_shape=[...]
where the time goes in v11:
time: 29.1 us; the launch traced here: 28.9 us
  Pallas kernels  28.3 us (97%)
  between operations  0.64 us (2%)
    pallas_call x1, Pallas kernels, per_device(): pl.pallas_call(functools.partial(kernel, plan, relay, width), out_shape=[...  27 us
    pallas_call x1, Pallas kernels, per_device(): pl.pallas_call(functools.partial(finish, dist), out_shape=[square] * 3, i...  1.26 us

profile of v11, /device:TPU:8, one launch (start us, length us, event | category | flops | bytes accessed | tf_op | source)
XLA Modules:
  0.0 28.9 jit_solution(5185708775000399411)
XLA Ops:
  0.6 27.0 %shard_map.85 = (f32[264,256]{1,0:T(8,128)S(1)}, f32[256,256]{1,0:T(8,128)S(1)}, f32[256,128]{1,0:T(8,128)S(1)}, f32[264,256]{1,0:T(8,128)S(1)}) custom-call(f32[7,256,256]{2,1,0:T(8,128)} %bitcast.9, f32[7,256,256]{2,1,0:T(8,128)} %bitcast.10, f32[7,256,256]{2,1,0:T(8,128)} %bitcast.11, s32[256,256]{1,0:T(8,128)} %bitcast.12, s32[1,256]{1,0:T(1,128)} %bitcast.13, ...), custom_call_target="tpu_custom_call" | custom-call | tf_op jit(solution)/shard_map/pallas_call | solution.py:624
  27.7 1.3 %shard_map.86 = (f32[256,256]{1,0:T(8,128)}, f32[256,256]{1,0:T(8,128)}, f32[256,256]{1,0:T(8,128)}) custom-call(f32[264,256]{1,0:T(8,128)S(1)} %get-tuple-element.10.acc, f32[256,256]{1,0:T(8,128)S(1)} %get-tuple-element.11.weight, f32[256,128]{1,0:T(8,128)S(1)} %get-tuple-element.12.row_sum, f32[264,256]{1,0:T(8,128)S(1)} %get-tuple-element.13.partial), custom_call_target="tpu_custom_call" | custom-call | tf_op jit(solution)/shard_map/pallas_call | solution.py:651

commit v12 on v11

--- a/solution.py
+++ b/solution.py
@@ -31,10 +31,10 @@
 )
 SPLIT = ()
 ORDER = {6: (1, 7, 6, 5, 4, 3, 2)}
-DETOUR = {(4, 7): (6, 7), (4, 6): (6, 2)}
+DETOUR = {(4, 7): (6, 5), (4, 6): (6, 4)}
 AFTER = {}
 FIRST = (7, 6, 11, 10, 4, 5, 9, 8, 2)
-SHARES = (8, 4, 3, 1)
+SHARES = (7, 5, 3, 1)
 CHUNKS = len(SHARES)
 COARSE = 2
 PIECES = 4
@@ -144,8 +144,10 @@
             start = sides[row, m][1]
             rows = pl.ds(start, SHARES[0] * unit - start)
         at = (m - 1, rows, pl.ds(0, half if (row, m) in halved else block))
-        slot = c if c < COARSE else COARSE + (c - COARSE) * dm + m - 1
-        return remote(qm.at[at], q_far.at[at], q_send.at[0], q_recv.at[slot], device)
+        slot = q_recv.at[c if c < CHUNKS - 1 else CHUNKS - 2 + m]
+        if COARSE <= c < CHUNKS - 1 and device >= live_rows:
+            slot = r_recv.at[m - 1]
+        return remote(qm.at[at], q_far.at[at], q_send.at[0], slot, device)
 
     def r_copy(m, device):
         return remote(qm1.at[dm - m], r_in.at[m - 1], r_send.at[0], r_recv.at[m - 1], device)
@@ -474,10 +476,11 @@
             far_list = far_list + jnp.where(me == device, listed(shifts), 0)
         for c in range(CHUNKS):
             at = rows_of(c)
-            if c < COARSE:
-                for count in sorted({units(row) for row in plan}):
-
-                    @pl.when(any_of(me, [plan[row][0] for row in plan if units(row) == count]))
+            if c < CHUNKS - 1:
+                whole_rows = [row for row in plan if c < COARSE or plan[row][0] < live_rows]
+                for count in sorted({units(row) for row in whole_rows}):
+
+                    @pl.when(any_of(me, [plan[row][0] for row in whole_rows if units(row) == count]))
                     def _():
                         whole = q_units(count, at)
                         remote(qm.at[whole], q_far.at[whole], q_send.at[0], q_recv.at[c], 0).wait_recv()
@@ -492,22 +495,29 @@
                         right = r_far[m]
                         rf_h[m], rf_l[m] = split(right)
                         column_sum(m, right, acc_far)
-                    if c >= COARSE:
-                        slot = q_recv.at[COARSE + (c - COARSE) * dm + m]
-
-                        def wait_for(lanes):
-                            here = (m, at, pl.ds(0, lanes))
-                            remote(qm.at[here], q_far.at[here], q_send.at[0], slot, 0).wait_recv()
-
+                    def wait_for(sem, lanes):
+                        here = (m, at, pl.ds(0, lanes))
+                        remote(qm.at[here], q_far.at[here], q_send.at[0], sem, 0).wait_recv()
+
+                    def wait_each(sem):
                         small = is_half(m, lambda row, _: plan[row][0])
 
                         @pl.when(small)
                         def _():
-                            wait_for(half)
+                            wait_for(sem, half)
 
                         @pl.when(jnp.logical_not(small))
                         def _():
-                            wait_for(block)
+                            wait_for(sem, block)
+
+                    if c == CHUNKS - 1:
+                        wait_each(q_recv.at[CHUNKS - 1 + m])
+                    elif c >= COARSE:
+
+                        @pl.when(jnp.logical_not(live))
+                        def _():
+                            wait_each(r_recv.at[m])
+
                     acc_far[rows_of(c, HEAD), :] += dot3(split(q_far[m, at, :]), (rf_h[m], rf_l[m]))
 
                 return rest // base
@@ -639,7 +649,7 @@
                 pltpu.VMEM((block, block), F32),
                 pltpu.VMEM((1, block), jnp.int32),
                 pltpu.VMEM((1, turner.shape[0]), F32),
-                dma((1,)), dma((1,)), dma((COARSE + (CHUNKS - COARSE) * dm,)), dma((1,)), dma((dm,)), dma((dm,)),
+                dma((1,)), dma((1,)), dma((CHUNKS - 1 + dm,)), dma((1,)), dma((dm,)), dma((dm,)),
                 dma((4,)), dma((2,)), dma((2,)),
                 pltpu.SemaphoreType.REGULAR((len(HELD),)),
             ],

time: 29.1 us -> 29 us (level)
  no operation moved by 1% of the time
where the time goes in v12:
time: 29 us; the launch traced here: 28.9 us
  Pallas kernels  28.2 us (97%)
  between operations  0.64 us (2%)
    pallas_call x1, Pallas kernels, per_device(): pl.pallas_call(functools.partial(kernel, plan, relay, width), out_shape=[...  27 us
    pallas_call x1, Pallas kernels, per_device(): pl.pallas_call(functools.partial(finish, dist), out_shape=[square] * 3, i...  1.26 us

profile of v12, /device:TPU:8, one launch (start us, length us, event | category | flops | bytes accessed | tf_op | source)
XLA Modules:
  0.0 28.9 jit_solution(1262065492789052705)
XLA Ops:
  0.6 27.0 %shard_map.85 = (f32[264,256]{1,0:T(8,128)S(1)}, f32[256,256]{1,0:T(8,128)S(1)}, f32[256,128]{1,0:T(8,128)S(1)}, f32[264,256]{1,0:T(8,128)S(1)}) custom-call(f32[7,256,256]{2,1,0:T(8,128)} %bitcast.9, f32[7,256,256]{2,1,0:T(8,128)} %bitcast.10, f32[7,256,256]{2,1,0:T(8,128)} %bitcast.11, s32[256,256]{1,0:T(8,128)} %bitcast.12, s32[1,256]{1,0:T(1,128)} %bitcast.13, ...), custom_call_target="tpu_custom_call" | custom-call | tf_op jit(solution)/shard_map/pallas_call | solution.py:634
  27.6 1.3 %shard_map.86 = (f32[256,256]{1,0:T(8,128)}, f32[256,256]{1,0:T(8,128)}, f32[256,256]{1,0:T(8,128)}) custom-call(f32[264,256]{1,0:T(8,128)S(1)} %get-tuple-element.10.acc, f32[256,256]{1,0:T(8,128)S(1)} %get-tuple-element.11.weight, f32[256,128]{1,0:T(8,128)S(1)} %get-tuple-element.12.row_sum, f32[264,256]{1,0:T(8,128)S(1)} %get-tuple-element.13.partial), custom_call_target="tpu_custom_call" | custom-call | tf_op jit(solution)/shard_map/pallas_call | solution.py:661

commit v13 on v12

--- a/solution.py
+++ b/solution.py
@@ -33,7 +33,7 @@
 ORDER = {6: (1, 7, 6, 5, 4, 3, 2)}
 DETOUR = {(4, 7): (6, 5), (4, 6): (6, 4)}
 AFTER = {}
-FIRST = (7, 6, 11, 10, 4, 5, 9, 8, 2)
+FIRST = (8, 11, 9, 10, 7, 4, 5, 6, 2)
 SHARES = (7, 5, 3, 1)
 CHUNKS = len(SHARES)
 COARSE = 2

time: 29 us -> 29.1 us (level)
  no operation moved by 1% of the time
where the time goes in v13:
time: 29.1 us; the launch traced here: 28.9 us
  Pallas kernels  28.2 us (97%)
  between operations  0.64 us (2%)
    pallas_call x1, Pallas kernels, per_device(): pl.pallas_call(functools.partial(kernel, plan, relay, width), out_shape=[...  27 us
    pallas_call x1, Pallas kernels, per_device(): pl.pallas_call(functools.partial(finish, dist), out_shape=[square] * 3, i...  1.26 us

profile of v13, /device:TPU:8, one launch (start us, length us, event | category | flops | bytes accessed | tf_op | source)
XLA Modules:
  0.0 28.9 jit_solution(13014548156538569537)
XLA Ops:
  0.6 27.0 %shard_map.85 = (f32[264,256]{1,0:T(8,128)S(1)}, f32[256,256]{1,0:T(8,128)S(1)}, f32[256,128]{1,0:T(8,128)S(1)}, f32[264,256]{1,0:T(8,128)S(1)}) custom-call(f32[7,256,256]{2,1,0:T(8,128)} %bitcast.9, f32[7,256,256]{2,1,0:T(8,128)} %bitcast.10, f32[7,256,256]{2,1,0:T(8,128)} %bitcast.11, s32[256,256]{1,0:T(8,128)} %bitcast.12, s32[1,256]{1,0:T(1,128)} %bitcast.13, ...), custom_call_target="tpu_custom_call" | custom-call | tf_op jit(solution)/shard_map/pallas_call | solution.py:634
  27.6 1.3 %shard_map.86 = (f32[256,256]{1,0:T(8,128)}, f32[256,256]{1,0:T(8,128)}, f32[256,256]{1,0:T(8,128)}) custom-call(f32[264,256]{1,0:T(8,128)S(1)} %get-tuple-element.10.acc, f32[256,256]{1,0:T(8,128)S(1)} %get-tuple-element.11.weight, f32[256,128]{1,0:T(8,128)S(1)} %get-tuple-element.12.row_sum, f32[264,256]{1,0:T(8,128)S(1)} %get-tuple-element.13.partial), custom_call_target="tpu_custom_call" | custom-call | tf_op jit(solution)/shard_map/pallas_call | solution.py:661

commit v14 on v13

--- a/solution.py
+++ b/solution.py
@@ -33,7 +33,7 @@
 ORDER = {6: (1, 7, 6, 5, 4, 3, 2)}
 DETOUR = {(4, 7): (6, 5), (4, 6): (6, 4)}
 AFTER = {}
-FIRST = (8, 11, 9, 10, 7, 4, 5, 6, 2)
+FIRST = (7, 4, 8, 11, 6, 5, 9, 10, 2)
 SHARES = (7, 5, 3, 1)
 CHUNKS = len(SHARES)
 COARSE = 2

time: 29.1 us -> 29.2 us (level)
  no operation moved by 1% of the time
where the time goes in v14:
time: 29.2 us; the launch traced here: 28.9 us
  Pallas kernels  28.3 us (97%)
  between operations  0.64 us (2%)
    pallas_call x1, Pallas kernels, per_device(): pl.pallas_call(functools.partial(kernel, plan, relay, width), out_shape=[...  27 us
    pallas_call x1, Pallas kernels, per_device(): pl.pallas_call(functools.partial(finish, dist), out_shape=[square] * 3, i...  1.26 us

profile of v14, /device:TPU:8, one launch (start us, length us, event | category | flops | bytes accessed | tf_op | source)
XLA Modules:
  0.0 28.9 jit_solution(10124973080078641591)
XLA Ops:
  0.6 27.0 %shard_map.85 = (f32[264,256]{1,0:T(8,128)S(1)}, f32[256,256]{1,0:T(8,128)S(1)}, f32[256,128]{1,0:T(8,128)S(1)}, f32[264,256]{1,0:T(8,128)S(1)}) custom-call(f32[7,256,256]{2,1,0:T(8,128)} %bitcast.9, f32[7,256,256]{2,1,0:T(8,128)} %bitcast.10, f32[7,256,256]{2,1,0:T(8,128)} %bitcast.11, s32[256,256]{1,0:T(8,128)} %bitcast.12, s32[1,256]{1,0:T(1,128)} %bitcast.13, ...), custom_call_target="tpu_custom_call" | custom-call | tf_op jit(solution)/shard_map/pallas_call | solution.py:634
  27.6 1.3 %shard_map.86 = (f32[256,256]{1,0:T(8,128)}, f32[256,256]{1,0:T(8,128)}, f32[256,256]{1,0:T(8,128)}) custom-call(f32[264,256]{1,0:T(8,128)S(1)} %get-tuple-element.10.acc, f32[256,256]{1,0:T(8,128)S(1)} %get-tuple-element.11.weight, f32[256,128]{1,0:T(8,128)S(1)} %get-tuple-element.12.row_sum, f32[264,256]{1,0:T(8,128)S(1)} %get-tuple-element.13.partial), custom_call_target="tpu_custom_call" | custom-call | tf_op jit(solution)/shard_map/pallas_call | solution.py:661

commit v15 on v12

--- a/solution.py
+++ b/solution.py
@@ -31,7 +31,7 @@
 )
 SPLIT = ()
 ORDER = {6: (1, 7, 6, 5, 4, 3, 2)}
-DETOUR = {(4, 7): (6, 5), (4, 6): (6, 4)}
+DETOUR = {(4, 7): (6, 5), (4, 6): (6, 5)}
 AFTER = {}
 FIRST = (7, 6, 11, 10, 4, 5, 9, 8, 2)
 SHARES = (7, 5, 3, 1)

time: 29 us -> 29.2 us (level); the launches traced: 28.9 us -> 28.6 us
  no operation moved by 1% of the time
where the time goes in v15:
time: 29.2 us; the launch traced here: 28.6 us
  Pallas kernels  28 us (96%)
  between operations  0.64 us (2%)
    pallas_call x1, Pallas kernels, per_device(): pl.pallas_call(functools.partial(kernel, plan, relay, width), out_shape=[...  26.7 us
    pallas_call x1, Pallas kernels, per_device(): pl.pallas_call(functools.partial(finish, dist), out_shape=[square] * 3, i...  1.26 us

profile of v15, /device:TPU:8, one launch (start us, length us, event | category | flops | bytes accessed | tf_op | source)
XLA Modules:
  0.0 28.6 jit_solution(5576412658004133802)
XLA Ops:
  0.6 26.7 %shard_map.85 = (f32[264,256]{1,0:T(8,128)S(1)}, f32[256,256]{1,0:T(8,128)S(1)}, f32[256,128]{1,0:T(8,128)S(1)}, f32[264,256]{1,0:T(8,128)S(1)}) custom-call(f32[7,256,256]{2,1,0:T(8,128)} %bitcast.9, f32[7,256,256]{2,1,0:T(8,128)} %bitcast.10, f32[7,256,256]{2,1,0:T(8,128)} %bitcast.11, s32[256,256]{1,0:T(8,128)} %bitcast.12, s32[1,256]{1,0:T(1,128)} %bitcast.13, ...), custom_call_target="tpu_custom_call" | custom-call | tf_op jit(solution)/shard_map/pallas_call | solution.py:634
  27.4 1.3 %shard_map.86 = (f32[256,256]{1,0:T(8,128)}, f32[256,256]{1,0:T(8,128)}, f32[256,256]{1,0:T(8,128)}) custom-call(f32[264,256]{1,0:T(8,128)S(1)} %get-tuple-element.10.acc, f32[256,256]{1,0:T(8,128)S(1)} %get-tuple-element.11.weight, f32[256,128]{1,0:T(8,128)S(1)} %get-tuple-element.12.row_sum, f32[264,256]{1,0:T(8,128)S(1)} %get-tuple-element.13.partial), custom_call_target="tpu_custom_call" | custom-call | tf_op jit(solution)/shard_map/pallas_call | solution.py:661
